TPU v7x, 512 devices: a whole 4x4x16 slice. The times are simulated.
512 devices in a mesh: space: 128 (over z, y, core), dp: 4 (over x).
Axes of the slice: x: 4, y: 4, z: 16, core: 2. Of those that a mesh axis runs over, the one named last changes fastest.
Arguments:
- features: bfloat16 [4, 512, 8, 8, 512], P('dp', 'space'), may hold values from -6 to 6
- occupancy: int32 [4, 512, 512], P('dp', 'space'), may hold values 0 or 1
- counts: int32 [4, 128], P('dp', 'space'), may hold values from 2 to 4, as said below
- send_units: int32 [4, 128, 5, 12], P('dp', 'space'), may hold values from -1 to 23, as said below
- neighbours: int32 [4, 512, 26], P('dp', 'space'), may hold values from -1 to 59, as said below
- weight: bfloat16 [1728, 64], P('dp'), may hold values from -0.15625 to 0.15625
- conv_bias: bfloat16 [64], P('dp'), may hold values from -3 to 3
- cotangent: bfloat16 [4, 512, 8, 8, 512], P('dp', 'space'), may hold values from -6 to 6
Outputs:
- block_output: bfloat16 [4, 512, 8, 8, 512], P('dp', 'space')
- grad_input: bfloat16 [4, 512, 8, 8, 512], P('dp', 'space')
- grad_weight: float32 [1728, 64], P('dp')
- grad_bias: float32 [64], P('dp')
Inputs may be any that keep to these rules, and one draw needn't show every extreme that they name: `counts`: each volume has a device holding 4 bricks. `send_units`: the entry of device q at j and l is -1 or 6 times a slot below counts of q plus ((j * 12 + l) mod 6); it is -1 where device q + j - 2 does not exist; link 0 is used wherever that device exists. `neighbours`: an entry n >= 0 of a brick on device r names a unit that device r + 2 - n // 12 sends, whose face is the one the entry's offset needs (2d if o_d = 1, 2d+1 if o_d = -1, d the first dimension where o is not 0).
All inputs are finite; a program needn't handle non-finite values. No bound on the sum of `occupancy` on one device may be relied on, other than what follows from the above.
Results may differ from a plain program's by a relative error of at most 0.012.
Values may be sent and summed in bfloat16 or wider, within the bound.
A program may use at most 64 MiB of HBM per device.

v0:
```python
import jax
import jax.numpy as jnp
from jax import lax
from jax.sharding import PartitionSpec as P


def passed_along(block, axis, distance):
    devices = range(lax.axis_size(axis))
    route = [(i - distance, i) for i in devices if i - distance in devices]
    return lax.ppermute(block, axis, route)


def neighbour_offsets():
    return [
        (first - 1, second - 1, third - 1)
        for first in range(3)
        for second in range(3)
        for third in range(3)
        if (first, second, third) != (1, 1, 1)
    ]


def first_moving(offset):
    for dimension in range(3):
        if offset[dimension] != 0:
            return dimension
    return 0


def face_planes(values):
    brick_edge = values.shape[1]
    planes = [
        values[:, 0],
        values[:, brick_edge - 1],
        values[:, :, 0],
        values[:, :, brick_edge - 1],
        values[:, :, :, 0],
        values[:, :, :, brick_edge - 1],
    ]
    return jnp.stack(planes, axis=1)


def rim_region(face_plane, offset, brick_edge):
    moving = first_moving(offset)
    region = face_plane
    other_dims = [dimension for dimension in range(3) if dimension != moving]
    for position, dimension in enumerate(other_dims):
        if offset[dimension] == -1:
            region = lax.slice_in_dim(region, brick_edge - 1, brick_edge, axis=position + 1)
        elif offset[dimension] == 1:
            region = lax.slice_in_dim(region, 0, 1, axis=position + 1)
    return jnp.expand_dims(region, moving + 1)


def halo_block(values, units, listing):
    brick_edge = values.shape[1]
    unit_total = units.shape[0]
    padded = jnp.pad(values, ((0, 0), (1, 1), (1, 1), (1, 1), (0, 0)))
    for offset_index, offset in enumerate(neighbour_offsets()):
        unit_index = listing[:, offset_index]
        face_plane = jnp.take(units, jnp.clip(unit_index, 0, unit_total - 1), axis=0)
        face_plane = face_plane * (unit_index >= 0).astype(face_plane.dtype)[:, None, None, None]
        region = rim_region(face_plane, offset, brick_edge)
        starts = (
            [0] + [0 if step == -1 else 1 if step == 0 else brick_edge + 1 for step in offset] + [0]
        )
        padded = lax.dynamic_update_slice(padded, region, starts)
    return padded


def share_faces(values, send_list):
    slot_count = values.shape[0]
    brick_edge = values.shape[1]
    channels = values.shape[-1]
    spread = send_list.shape[0]
    link_count = send_list.shape[1]
    reach_span = (spread - 1) // 2
    flattened = face_planes(values).reshape(slot_count * 6, brick_edge, brick_edge * channels)
    picked = jnp.take(flattened, jnp.clip(send_list, 0, slot_count * 6 - 1).reshape(-1), axis=0)
    picked = picked * (send_list.reshape(-1) >= 0).astype(values.dtype)[:, None, None]
    outgoing = picked.reshape(spread, link_count, brick_edge, brick_edge * channels)
    pieces = [None] * spread
    pieces[reach_span] = outgoing[reach_span]
    for column in range(spread):
        if column != reach_span:
            pieces[column] = passed_along(outgoing[column], "space", column - reach_span)
    received = jnp.stack(pieces)
    return received.reshape(spread * link_count, brick_edge, brick_edge, channels)


def windows(padded, brick_edge):
    return [
        padded[
            :,
            first : first + brick_edge,
            second : second + brick_edge,
            third : third + brick_edge,
            :,
        ]
        for first in range(3)
        for second in range(3)
        for third in range(3)
    ]


def gathered_columns(brick_block, brick_edge):
    return jnp.concatenate(
        [window.reshape(-1, window.shape[-1]) for window in windows(brick_block[None], brick_edge)],
        axis=1,
    )


def convolve(padded, kernels, brick_edge):
    stacked_kernel = kernels.reshape(-1, kernels.shape[-1])

    def convolve_per_brick(brick_block):
        return jnp.dot(
            gathered_columns(brick_block, brick_edge),
            stacked_kernel,
            preferred_element_type=jnp.float32,
        )

    result = lax.map(convolve_per_brick, padded)
    return result.reshape(padded.shape[0], brick_edge, brick_edge, brick_edge, -1)


def weight_terms(padded, grads, brick_edge):
    channels = padded.shape[-1]

    def weight_per_brick(running_total, brick_pair):
        brick_block, grad_block = brick_pair
        product = lax.dot_general(
            gathered_columns(brick_block, brick_edge),
            grad_block.reshape(-1, channels),
            (((0,), (0,)), ((), ())),
            preferred_element_type=jnp.float32,
        )
        return (running_total + product, None)

    running_total, unused_out = lax.scan(
        weight_per_brick, jnp.zeros((27 * channels, channels), jnp.float32), (padded, grads)
    )
    return running_total


def body(features, occupancy, counts, send_units, neighbours, weight, conv_bias, cotangent):
    slot_count = features.shape[1]
    brick_edge = features.shape[2]
    channels = features.shape[4] // brick_edge
    shard_shape = features.shape
    grid_shape = (slot_count, brick_edge, brick_edge, brick_edge, channels)
    listing = neighbours[0]
    send_list = send_units[0, 0]
    live_slot = (jnp.arange(slot_count, dtype=jnp.int32) < counts[0, 0]).astype(jnp.int32)
    active = (occupancy[0] * live_slot[:, None]).reshape(
        slot_count, brick_edge, brick_edge, brick_edge, 1
    )
    active_full = active.astype(jnp.float32)
    weight_all, bias_all = (
        lax.all_gather(weight, "dp", axis=0, tiled=True),
        lax.all_gather(conv_bias, "dp", axis=0, tiled=True),
    )
    kernels = weight_all.reshape(27, channels, channels)
    masked = features[0].reshape(grid_shape) * active.astype(jnp.bfloat16)
    padded_input = halo_block(masked, share_faces(masked, send_list), listing)
    pre_activation = convolve(padded_input, kernels, brick_edge) + bias_all.astype(jnp.float32)
    sigmoid_pre = jax.nn.sigmoid(pre_activation)
    block_output = (pre_activation * sigmoid_pre * active_full).astype(jnp.bfloat16)
    grad_pre = (
        cotangent[0].reshape(grid_shape).astype(jnp.float32)
        * sigmoid_pre
        * (1.0 + pre_activation * (1.0 - sigmoid_pre))
        * active_full
    ).astype(jnp.bfloat16)
    padded_grad = halo_block(grad_pre, share_faces(grad_pre, send_list), listing)
    mirrored = jnp.swapaxes(kernels[::-1], 1, 2)
    grad_input = (convolve(padded_grad, mirrored, brick_edge) * active_full).astype(jnp.bfloat16)
    weight_grad = weight_terms(padded_input, grad_pre, brick_edge)
    bias_grad = jnp.sum(grad_pre.astype(jnp.float32).reshape(-1, channels), axis=0)
    weight_total, bias_total = lax.psum((weight_grad, bias_grad), "space")
    weight_share, bias_share = (
        lax.psum_scatter(
            weight_total.astype(jnp.bfloat16), "dp", scatter_dimension=0, tiled=True
        ).astype(jnp.float32),
        lax.psum_scatter(
            bias_total.astype(jnp.bfloat16), "dp", scatter_dimension=0, tiled=True
        ).astype(jnp.float32),
    )
    return (
        block_output.reshape(shard_shape),
        grad_input.reshape(shard_shape),
        weight_share,
        bias_share,
    )


def solution(mesh):
    placed = (
        P("dp", "space", None, None, None),
        P("dp", "space", None),
        P("dp", "space"),
        P("dp", "space", None, None),
        P("dp", "space", None),
        P("dp", None),
        P("dp"),
        P("dp", "space", None, None, None),
    )
    return jax.shard_map(
        body,
        mesh=mesh,
        in_specs=placed,
        out_specs=(
            P("dp", "space", None, None, None),
            P("dp", "space", None, None, None),
            P("dp", None),
            P("dp"),
        ),
        check_vma=False,
    )
```

profile of v0, /device:TPU:1, one launch (start us, length us, event | category | flops | bytes accessed | tf_op | source)
XLA Modules:
  0.0 860.6 jit_solution(1383428674830892862)
XLA Ops:
  13.4 1.4 collective-permute-start
  14.8 8.7 %collective-permute-start.1 = (bf16[12,8,512]{2,1,0:T(8,128)(2,1)}, bf16[12,8,512]{2,1,0:T(8,128)(2,1)}, u32[]{:S(2)}, u32[]{:S(2)}) collective-permute-start(bf16[12,8,512]{2,1,0:T(8,128)(2,1)} %get-tuple-element.302), channel_id=1, source_target_pairs={{4,0},{8,4},{12,8},{16,12},{20,16},{24,20},{28,24},{32,28},{36,32}... | collective-permute-start | bytes 294920 | tf_op jit(solution)/shard_map/ppermute | solution.py:10
  23.6 4.2 collective-permute-start.2
  27.7 2.7 collective-permute-start.3
  56.8 9.4 %all-gather = bf16[4,432,64]{1,2,0:T(8,128)(2,1)S(1)} all-gather(bf16[1,432,64]{1,2,0:T(8,128)(2,1)S(1)} %bitcast.603), channel_id=1, replica_groups=mesh['space'=128,'dp'=4] {'dp'}, dimensions={0}, use_global_device_ids=true | all-gather | bytes 276480 | tf_op jit(solution)/shard_map/all_gather | solution.py:160
  70.7 6.4 all-reduce.2
  80.2 1.7 reshape.798
  113.9 1.3 gather_fusion.24
  128.5 2.8 dynamic_update_slice.175
  131.3 2.8 dynamic_update_slice.176
  143.1 34.4 %while.31 = (s32[]{:T(128)}, f32[4,512,64]{1,2,0:T(8,128)}, bf16[4,10,10,10,64]{4,3,2,1,0:T(8,128)(2,1)S(1)}, bf16[1728,64]{1,0:T(8,128)(2,1)}, s32[]{:T(128)}, /*index=5*/s32[]{:T(128)}, s32[]{}, s32[]{}) while((s32[]{:T(128)}, f32[4,512,64]{1,2,0:T(8,128)}, bf16[4,10,10,10,64]{4,3,2,1,0:T(8,128)(2,1)S(1)}, bf16[1728,64]{1,0:T(8,128)(2,1)}, ...), condition=%wide.region_1.4_spmd, body=%wide.region_0.0_spmd.sunk | while | flops 113246208 | bytes 9421433 | solution.py:123
  143.1 2.1 constant_dynamic-slice_fusion.85
  145.2 4.2 concatenate.13
  149.4 2.3 fusion.84
  151.7 2.1 constant_dynamic-slice_fusion.85
  153.8 4.2 concatenate.13
  158.0 2.3 fusion.84
  160.3 2.1 constant_dynamic-slice_fusion.85
  162.4 4.2 concatenate.13
  166.6 2.3 fusion.84
  168.9 2.1 constant_dynamic-slice_fusion.85
  171.0 4.2 concatenate.13
  175.2 2.4 fusion.84
  177.5 1.4 copy.428
  179.0 2.1 multiply_convert_fusion
  183.0 2.3 reshape.794
  185.3 44.5 %while.33 = (s32[]{:T(128)}, f32[1728,64]{0,1:T(8,128)}, bf16[4,10,10,10,64]{4,3,2,1,0:T(8,128)(2,1)S(1)}, bf16[4,8,8,8,64]{4,3,2,1,0:T(8,128)(2,1)}, s32[]{:T(128)}, /*index=5*/s32[]{:T(128)}, s32[]{}, s32[]{}) while((s32[]{:T(128)}, f32[1728,64]{0,1:T(8,128)}, bf16[4,10,10,10,64]{4,3,2,1,0:T(8,128)(2,1)S(1)}, ...), condition=%wide.region_5.8_spmd.clone, body=%wide.region_4.7_spmd.clone.sunk | while | flops 113467392 | bytes 9928835 | solution.py:140
  185.3 3.0 constant_dynamic-slice_fusion.87
  188.4 5.3 concatenate.15
  193.6 2.8 convolution_add_fusion.2
  196.4 3.0 constant_dynamic-slice_fusion.87
  199.5 5.3 concatenate.15
  204.7 2.8 convolution_add_fusion.2
  207.6 3.0 constant_dynamic-slice_fusion.87
  210.6 5.3 concatenate.15
  215.9 2.8 convolution_add_fusion.2
  218.7 3.0 constant_dynamic-slice_fusion.87
  221.7 5.3 concatenate.15
  227.0 2.8 convolution_add_fusion.2
  231.0 1.5 convert_reduce_fusion
  232.5 493.7 %all-reduce.6 = (bf16[1728,64]{0,1:T(8,128)(2,1)S(1)}, bf16[64]{0:T(256)(128)(2,1)S(1)}) all-reduce(f32[1728,64]{0,1:T(8,128)S(1)} %copy-done, f32[64]{0:T(128)S(1)} %convert_reduce_fusion), channel_id=1, replica_groups=mesh['space'=128,'dp'=4] {'space'}, use_global_device_ids=true, to_apply=%region_6.9 | all-reduce | flops 110656 | bytes 663936 | tf_op jit(solution)/shard_map/psum | solution.py:180
  727.2 6.0 all-reduce.3
  738.4 9.3 %collective-permute-start.5 = (bf16[12,8,512]{2,1,0:T(8,128)(2,1)S(1)}, bf16[12,8,512]{2,1,0:T(8,128)(2,1)S(1)}, u32[]{:S(2)}, u32[]{:S(2)}) collective-permute-start(bf16[12,8,512]{2,1,0:T(8,128)(2,1)S(1)} %get-tuple-element.298), channel_id=1, source_target_pairs={{4,0},{8,4},{12,8},{16,12},{20,16},{24,20},{28,24},{32,28},{36,32}... | collective-permute-start | bytes 294920 | tf_op jit(solution)/shard_map/ppermute | solution.py:10
  747.7 4.2 collective-permute-start.6
  751.9 2.0 collective-permute-start.7
  757.4 1.4 gather_fusion.29
  764.8 1.3 gather_fusion.36
  772.9 1.3 gather_fusion.46
  802.9 2.8 dynamic_update_slice.201
  805.7 2.8 dynamic_update_slice.202
  810.7 38.6 %while.32 = (s32[]{:T(128)}, f32[4,512,64]{1,2,0:T(8,128)}, bf16[4,10,10,10,64]{4,3,2,1,0:T(8,128)(2,1)S(1)}, bf16[1728,64]{1,0:T(8,128)(2,1)S(1)}, s32[]{:T(128)}, /*index=5*/s32[]{:T(128)}, s32[]{}, s32[]{}) while((s32[]{:T(128)}, f32[4,512,64]{1,2,0:T(8,128)}, bf16[4,10,10,10,64]{4,3,2,1,0:T(8,128)(2,1)S(1)}, ...), condition=%wide.region_3.6_spmd, body=%wide.region_2.5_spmd.sunk | while | flops 113246208 | bytes 9265785 | solution.py:123
  810.7 1.9 constant_dynamic-slice_fusion.86
  812.5 5.0 concatenate.14
  817.5 2.8 fusion.87
  820.3 1.9 constant_dynamic-slice_fusion.86
  822.2 5.0 concatenate.14
  827.1 2.8 fusion.87
  830.0 1.9 constant_dynamic-slice_fusion.86
  831.8 5.0 concatenate.14
  836.8 2.8 fusion.87
  839.6 1.9 constant_dynamic-slice_fusion.86
  841.5 5.0 concatenate.14
  846.4 2.8 fusion.87
  849.3 1.5 copy.463
  (498 shorter events, 149.7 us)
Async XLA Ops:
  7.2 844.9 %reduce-scatter.4.cloned.1.call-start = ((), (), s32[]{:S(2)}) async-start(), calls=%async_computation.1 | async-start | bytes 552960
  10.0 73.6 %copy-start.8 = (f32[4,8,8,8]{3,2,1,0:T(8,128)}, f32[4,8,8,8]{3,2,1,0:T(8,128)S(1)}, u32[]{:S(2)}) copy-start(f32[4,8,8,8]{3,2,1,0:T(8,128)S(1)} %get-tuple-element.305) | copy-start | bytes 24580
  10.9 19.5 %copy-start.4 = (s32[1,4,26]{2,1,0:T(4,128)S(1)}, s32[1,4,26]{2,1,0:T(4,128)}, u32[]{:S(2)}) copy-start(s32[1,4,26]{2,1,0:T(4,128)} %param.22) | copy-start | bytes 1252
  11.2 44.2 %copy-start.10 = (bf16[1,4,8,8,512]{4,3,2,1,0:T(8,128)(2,1)S(1)}, bf16[1,4,8,8,512]{4,3,2,1,0:T(8,128)(2,1)}, u32[]{:S(2)}) copy-start(bf16[1,4,8,8,512]{4,3,2,1,0:T(8,128)(2,1)} %param.25) | copy-start | bytes 786436
  12.6 44.2 %copy-start.7 = (bf16[60,8,512]{2,1,0:T(8,128)(2,1)}, bf16[60,8,512]{2,1,0:T(8,128)(2,1)S(1)}, u32[]{:S(2)}) copy-start(bf16[60,8,512]{2,1,0:T(8,128)(2,1)S(1)} %select_multiply_fusion.1) | copy-start | bytes 1474564
  13.4 43.5 %copy-start.14 = (bf16[432,64]{0,1:T(8,128)(2,1)S(1)}, bf16[432,64]{0,1:T(8,128)(2,1)}, u32[]{:S(2)}) copy-start(bf16[432,64]{0,1:T(8,128)(2,1)} %param.23) | copy-start | bytes 165892
  13.4 74.8 %collective-permute-start = (bf16[12,8,512]{2,1,0:T(8,128)(2,1)}, bf16[12,8,512]{2,1,0:T(8,128)(2,1)}, u32[]{:S(2)}, u32[]{:S(2)}) collective-permute-start(bf16[12,8,512]{2,1,0:T(8,128)(2,1)} %get-tuple-element.303), channel_id=1, source_target_pairs={{8,0},{12,4},{16,8},{20,12},{24,16},{28,20},{32,24},{36,28},{40,32... | collective-permute-start | bytes 294920 | tf_op jit(solution)/shard_map/ppermute | solution.py:10
  14.8 74.2 %collective-permute-start.1 = (bf16[12,8,512]{2,1,0:T(8,128)(2,1)}, bf16[12,8,512]{2,1,0:T(8,128)(2,1)}, u32[]{:S(2)}, u32[]{:S(2)}) collective-permute-start(bf16[12,8,512]{2,1,0:T(8,128)(2,1)} %get-tuple-element.302), channel_id=1, source_target_pairs={{4,0},{8,4},{12,8},{16,12},{20,16},{24,20},{28,24},{32,28},{36,32}... | collective-permute-start | bytes 294920 | tf_op jit(solution)/shard_map/ppermute | solution.py:10
  23.6 67.3 %collective-permute-start.2 = (bf16[12,8,512]{2,1,0:T(8,128)(2,1)S(1)}, bf16[12,8,512]{2,1,0:T(8,128)(2,1)}, u32[]{:S(2)}, u32[]{:S(2)}) collective-permute-start(bf16[12,8,512]{2,1,0:T(8,128)(2,1)S(1)} %get-tuple-element.301), channel_id=1, source_target_pairs={{0,4},{4,8},{8,12},{12,16},{16,20},{20,24},{24,28},{28,32},{32,36}... | collective-permute-start | bytes 294920 | tf_op jit(solution)/shard_map/ppermute | solution.py:10
  27.7 64.0 %collective-permute-start.3 = (bf16[12,8,512]{2,1,0:T(8,128)(2,1)S(1)}, bf16[12,8,512]{2,1,0:T(8,128)(2,1)}, u32[]{:S(2)}, u32[]{:S(2)}) collective-permute-start(bf16[12,8,512]{2,1,0:T(8,128)(2,1)S(1)} %get-tuple-element.300), channel_id=1, source_target_pairs={{0,8},{4,12},{8,16},{12,20},{16,24},{20,28},{24,32},{28,36},{32,40... | collective-permute-start | bytes 294920 | tf_op jit(solution)/shard_map/ppermute | solution.py:10
  85.7 12.2 %copy-start.20 = (s32[1024]{0:T(1024)}, s32[1024]{0:T(1024)S(1)}, u32[]{:S(2)}) copy-start(s32[1024]{0:T(1024)S(1)} %get-tuple-element.332) | copy-start | bytes 12292
  85.7 12.2 %copy-start.21 = (s32[1024]{0:T(1024)}, s32[1024]{0:T(1024)S(1)}, u32[]{:S(2)}) copy-start(s32[1024]{0:T(1024)S(1)} %get-tuple-element.333) | copy-start | bytes 12292
  85.8 12.1 %copy-start.22 = (s32[1024]{0:T(1024)}, s32[1024]{0:T(1024)S(1)}, u32[]{:S(2)}) copy-start(s32[1024]{0:T(1024)S(1)} %get-tuple-element.330) | copy-start | bytes 12292
  85.8 13.8 %copy-start.24 = (s32[1024]{0:T(1024)}, s32[1024]{0:T(1024)S(1)}, u32[]{:S(2)}) copy-start(s32[1024]{0:T(1024)S(1)} %get-tuple-element.328) | copy-start | bytes 12292
  85.9 13.8 %copy-start.25 = (s32[1024]{0:T(1024)}, s32[1024]{0:T(1024)S(1)}, u32[]{:S(2)}) copy-start(s32[1024]{0:T(1024)S(1)} %get-tuple-element.329) | copy-start | bytes 12292
  85.9 13.8 %copy-start.27 = (s32[1024]{0:T(1024)}, s32[1024]{0:T(1024)S(1)}, u32[]{:S(2)}) copy-start(s32[1024]{0:T(1024)S(1)} %get-tuple-element.327) | copy-start | bytes 12292
  85.9 15.0 %copy-start.26 = (s32[1024]{0:T(1024)}, s32[1024]{0:T(1024)S(1)}, u32[]{:S(2)}) copy-start(s32[1024]{0:T(1024)S(1)} %get-tuple-element.326) | copy-start | bytes 12292
  86.0 16.1 %copy-start.29 = (s32[1024]{0:T(1024)}, s32[1024]{0:T(1024)S(1)}, u32[]{:S(2)}) copy-start(s32[1024]{0:T(1024)S(1)} %get-tuple-element.325) | copy-start | bytes 12292
  86.0 17.2 %copy-start.28 = (s32[1024]{0:T(1024)}, s32[1024]{0:T(1024)S(1)}, u32[]{:S(2)}) copy-start(s32[1024]{0:T(1024)S(1)} %get-tuple-element.324) | copy-start | bytes 12292
  86.0 17.8 %copy-start.31 = (s32[1024]{0:T(1024)}, s32[1024]{0:T(1024)S(1)}, u32[]{:S(2)}) copy-start(s32[1024]{0:T(1024)S(1)} %get-tuple-element.323) | copy-start | bytes 12292
  86.0 18.3 %copy-start.30 = (s32[1024]{0:T(1024)}, s32[1024]{0:T(1024)S(1)}, u32[]{:S(2)}) copy-start(s32[1024]{0:T(1024)S(1)} %get-tuple-element.322) | copy-start | bytes 12292
  86.1 18.9 %copy-start.33 = (s32[1024]{0:T(1024)}, s32[1024]{0:T(1024)S(1)}, u32[]{:S(2)}) copy-start(s32[1024]{0:T(1024)S(1)} %get-tuple-element.321) | copy-start | bytes 12292
  86.1 19.7 %copy-start.32 = (s32[1024]{0:T(1024)}, s32[1024]{0:T(1024)S(1)}, u32[]{:S(2)}) copy-start(s32[1024]{0:T(1024)S(1)} %get-tuple-element.320) | copy-start | bytes 12292
  86.1 20.4 %copy-start.35 = (s32[1024]{0:T(1024)}, s32[1024]{0:T(1024)S(1)}, u32[]{:S(2)}) copy-start(s32[1024]{0:T(1024)S(1)} %get-tuple-element.319) | copy-start | bytes 12292
  86.1 21.0 %copy-start.34 = (s32[1024]{0:T(1024)}, s32[1024]{0:T(1024)S(1)}, u32[]{:S(2)}) copy-start(s32[1024]{0:T(1024)S(1)} %get-tuple-element.318) | copy-start | bytes 12292
  86.2 21.5 %copy-start.37 = (s32[1024]{0:T(1024)}, s32[1024]{0:T(1024)S(1)}, u32[]{:S(2)}) copy-start(s32[1024]{0:T(1024)S(1)} %get-tuple-element.317) | copy-start | bytes 12292
  86.2 22.1 %copy-start.36 = (s32[1024]{0:T(1024)}, s32[1024]{0:T(1024)S(1)}, u32[]{:S(2)}) copy-start(s32[1024]{0:T(1024)S(1)} %get-tuple-element.316) | copy-start | bytes 12292
  86.2 23.2 %copy-start.39 = (s32[1024]{0:T(1024)}, s32[1024]{0:T(1024)S(1)}, u32[]{:S(2)}) copy-start(s32[1024]{0:T(1024)S(1)} %get-tuple-element.315) | copy-start | bytes 12292
  86.2 24.4 %copy-start.38 = (s32[1024]{0:T(1024)}, s32[1024]{0:T(1024)S(1)}, u32[]{:S(2)}) copy-start(s32[1024]{0:T(1024)S(1)} %get-tuple-element.314) | copy-start | bytes 12292
  92.7 12.8 %copy-start.42 = (bf16[4]{0:T(256)(128)(2,1)S(1)}, bf16[4]{0:T(256)(128)(2,1)}, u32[]{:S(2)}) copy-start(bf16[4]{0:T(256)(128)(2,1)} %get-tuple-element.143) | copy-start | bytes 28
  92.7 12.8 %copy-start.52 = (pred[4]{0:T(512)(128)(4,1)S(1)}, pred[4]{0:T(512)(128)(4,1)}, u32[]{:S(2)}) copy-start(pred[4]{0:T(512)(128)(4,1)} %get-tuple-element.353) | copy-start | bytes 16
  92.7 13.6 %copy-start.41 = (bf16[4]{0:T(256)(128)(2,1)S(1)}, bf16[4]{0:T(256)(128)(2,1)}, u32[]{:S(2)}) copy-start(bf16[4]{0:T(256)(128)(2,1)} %get-tuple-element.144) | copy-start | bytes 28
  92.7 13.6 %copy-start.49 = (pred[4]{0:T(512)(128)(4,1)S(1)}, pred[4]{0:T(512)(128)(4,1)}, u32[]{:S(2)}) copy-start(pred[4]{0:T(512)(128)(4,1)} %get-tuple-element.352) | copy-start | bytes 16
  117.5 18.4 %copy-start.40 = (bf16[4]{0:T(256)(128)(2,1)S(1)}, bf16[4]{0:T(256)(128)(2,1)}, u32[]{:S(2)}) copy-start(bf16[4]{0:T(256)(128)(2,1)} %get-tuple-element.147) | copy-start | bytes 28
  117.5 18.4 %copy-start.48 = (pred[4]{0:T(512)(128)(4,1)S(1)}, pred[4]{0:T(512)(128)(4,1)}, u32[]{:S(2)}) copy-start(pred[4]{0:T(512)(128)(4,1)} %get-tuple-element.349) | copy-start | bytes 16
  117.5 18.8 %copy-start.55 = (bf16[4]{0:T(256)(128)(2,1)S(1)}, bf16[4]{0:T(256)(128)(2,1)}, u32[]{:S(2)}) copy-start(bf16[4]{0:T(256)(128)(2,1)} %get-tuple-element.148) | copy-start | bytes 28
  117.5 18.8 %copy-start.61 = (pred[4]{0:T(512)(128)(4,1)S(1)}, pred[4]{0:T(512)(128)(4,1)}, u32[]{:S(2)}) copy-start(pred[4]{0:T(512)(128)(4,1)} %get-tuple-element.348) | copy-start | bytes 16
  117.6 19.6 %copy-start.60 = (bf16[4]{0:T(256)(128)(2,1)S(1)}, bf16[4]{0:T(256)(128)(2,1)}, u32[]{:S(2)}) copy-start(bf16[4]{0:T(256)(128)(2,1)} %get-tuple-element.169) | copy-start | bytes 28
  117.6 19.6 %copy-start.63 = (pred[4]{0:T(512)(128)(4,1)S(1)}, pred[4]{0:T(512)(128)(4,1)}, u32[]{:S(2)}) copy-start(pred[4]{0:T(512)(128)(4,1)} %get-tuple-element.347) | copy-start | bytes 16
  117.6 20.5 %copy-start.59 = (bf16[4]{0:T(256)(128)(2,1)S(1)}, bf16[4]{0:T(256)(128)(2,1)}, u32[]{:S(2)}) copy-start(bf16[4]{0:T(256)(128)(2,1)} %get-tuple-element.170) | copy-start | bytes 28
  117.6 20.5 %copy-start.62 = (pred[4]{0:T(512)(128)(4,1)S(1)}, pred[4]{0:T(512)(128)(4,1)}, u32[]{:S(2)}) copy-start(pred[4]{0:T(512)(128)(4,1)} %get-tuple-element.346) | copy-start | bytes 16
  117.6 21.3 %copy-start.45 = (bf16[4]{0:T(256)(128)(2,1)S(1)}, bf16[4]{0:T(256)(128)(2,1)}, u32[]{:S(2)}) copy-start(bf16[4]{0:T(256)(128)(2,1)} %get-tuple-element.171) | copy-start | bytes 28
  117.6 21.3 %copy-start.53 = (pred[4]{0:T(512)(128)(4,1)S(1)}, pred[4]{0:T(512)(128)(4,1)}, u32[]{:S(2)}) copy-start(pred[4]{0:T(512)(128)(4,1)} %get-tuple-element.345) | copy-start | bytes 16
  117.6 21.5 %copy-start.44 = (bf16[4]{0:T(256)(128)(2,1)S(1)}, bf16[4]{0:T(256)(128)(2,1)}, u32[]{:S(2)}) copy-start(bf16[4]{0:T(256)(128)(2,1)} %get-tuple-element.172) | copy-start | bytes 28
  117.6 21.5 %copy-start.50 = (pred[4]{0:T(512)(128)(4,1)S(1)}, pred[4]{0:T(512)(128)(4,1)}, u32[]{:S(2)}) copy-start(pred[4]{0:T(512)(128)(4,1)} %get-tuple-element.344) | copy-start | bytes 16
  117.6 21.9 %copy-start.43 = (bf16[4]{0:T(256)(128)(2,1)S(1)}, bf16[4]{0:T(256)(128)(2,1)}, u32[]{:S(2)}) copy-start(bf16[4]{0:T(256)(128)(2,1)} %get-tuple-element.173) | copy-start | bytes 28
  117.6 21.9 %copy-start.51 = (pred[4]{0:T(512)(128)(4,1)S(1)}, pred[4]{0:T(512)(128)(4,1)}, u32[]{:S(2)}) copy-start(pred[4]{0:T(512)(128)(4,1)} %get-tuple-element.343) | copy-start | bytes 16
  117.7 22.1 %copy-start.58 = (bf16[4]{0:T(256)(128)(2,1)S(1)}, bf16[4]{0:T(256)(128)(2,1)}, u32[]{:S(2)}) copy-start(bf16[4]{0:T(256)(128)(2,1)} %get-tuple-element.174) | copy-start | bytes 28
  117.7 22.1 %copy-start.64 = (pred[4]{0:T(512)(128)(4,1)S(1)}, pred[4]{0:T(512)(128)(4,1)}, u32[]{:S(2)}) copy-start(pred[4]{0:T(512)(128)(4,1)} %get-tuple-element.342) | copy-start | bytes 16
  117.7 22.9 %copy-start.57 = (bf16[4]{0:T(256)(128)(2,1)S(1)}, bf16[4]{0:T(256)(128)(2,1)}, u32[]{:S(2)}) copy-start(bf16[4]{0:T(256)(128)(2,1)} %get-tuple-element.168) | copy-start | bytes 28
  117.7 22.9 %copy-start.66 = (pred[4]{0:T(512)(128)(4,1)S(1)}, pred[4]{0:T(512)(128)(4,1)}, u32[]{:S(2)}) copy-start(pred[4]{0:T(512)(128)(4,1)} %get-tuple-element.341) | copy-start | bytes 16
  117.7 23.7 %copy-start.54 = (bf16[4]{0:T(256)(128)(2,1)S(1)}, bf16[4]{0:T(256)(128)(2,1)}, u32[]{:S(2)}) copy-start(bf16[4]{0:T(256)(128)(2,1)} %get-tuple-element.130) | copy-start | bytes 28
  117.7 23.7 %copy-start.65 = (pred[4]{0:T(512)(128)(4,1)S(1)}, pred[4]{0:T(512)(128)(4,1)}, u32[]{:S(2)}) copy-start(pred[4]{0:T(512)(128)(4,1)} %get-tuple-element.340) | copy-start | bytes 16
  143.1 35.9 %copy-start.67 = (f32[64]{0:T(128)S(1)}, f32[64]{0:T(128)}, u32[]{:S(2)}) copy-start(f32[64]{0:T(128)} %convert_element_type.451) | copy-start | bytes 772
  229.9 503.4 %copy-start.11 = (bf16[4,6,8,8,64]{4,3,2,1,0:T(8,128)(2,1)S(1)}, bf16[4,6,8,8,64]{4,3,2,1,0:T(8,128)(2,1)}, u32[]{:S(2)}) copy-start(bf16[4,6,8,8,64]{4,3,2,1,0:T(8,128)(2,1)} %slice_dynamic-update-slice_fusion.1) | copy-start | bytes 589828
  231.0 504.8 %copy-start.13 = (bf16[4,8,8,1,64]{4,3,2,1,0:T(2,128)(2,1)S(1)}, bf16[4,8,8,1,64]{4,3,2,1,0:T(2,128)(2,1)}, u32[]{:S(2)}) copy-start(bf16[4,8,8,1,64]{4,3,2,1,0:T(2,128)(2,1)} %get-tuple-element.293) | copy-start | bytes 98308
  231.0 504.8 %copy-start.12 = (bf16[4,8,8,1,64]{4,3,2,1,0:T(2,128)(2,1)S(1)}, bf16[4,8,8,1,64]{4,3,2,1,0:T(2,128)(2,1)}, u32[]{:S(2)}) copy-start(bf16[4,8,8,1,64]{4,3,2,1,0:T(2,128)(2,1)} %get-tuple-element.292) | copy-start | bytes 98308
  737.1 17.4 %collective-permute-start.4 = (bf16[12,8,512]{2,1,0:T(8,128)(2,1)S(1)}, bf16[12,8,512]{2,1,0:T(8,128)(2,1)S(1)}, u32[]{:S(2)}, u32[]{:S(2)}) collective-permute-start(bf16[12,8,512]{2,1,0:T(8,128)(2,1)S(1)} %get-tuple-element.299), channel_id=1, source_target_pairs={{8,0},{12,4},{16,8},{20,12},{24,16},{28,20},{32,24},{36,28},{40,32... | collective-permute-start | bytes 294920 | tf_op jit(solution)/shard_map/ppermute | solution.py:10
  738.4 16.1 %collective-permute-start.5 = (bf16[12,8,512]{2,1,0:T(8,128)(2,1)S(1)}, bf16[12,8,512]{2,1,0:T(8,128)(2,1)S(1)}, u32[]{:S(2)}, u32[]{:S(2)}) collective-permute-start(bf16[12,8,512]{2,1,0:T(8,128)(2,1)S(1)} %get-tuple-element.298), channel_id=1, source_target_pairs={{4,0},{8,4},{12,8},{16,12},{20,16},{24,20},{28,24},{32,28},{36,32}... | collective-permute-start | bytes 294920 | tf_op jit(solution)/shard_map/ppermute | solution.py:10
  747.7 6.9 collective-permute-start.6
  751.9 3.6 collective-permute-start.7
  757.4 23.9 %copy-start.56 = (bf16[4]{0:T(256)(128)(2,1)S(1)}, bf16[4]{0:T(256)(128)(2,1)}, u32[]{:S(2)}) copy-start(bf16[4]{0:T(256)(128)(2,1)} %get-tuple-element.131) | copy-start | bytes 28
  757.4 23.9 %copy-start.70 = (pred[4]{0:T(512)(128)(4,1)S(1)}, pred[4]{0:T(512)(128)(4,1)}, u32[]{:S(2)}) copy-start(pred[4]{0:T(512)(128)(4,1)} %compare_and_fusion.25) | copy-start | bytes 16
  789.0 21.7 %copy-start.1 = (bf16[27,64,64]{2,1,0:T(8,128)(2,1)S(1)}, bf16[27,64,64]{2,1,0:T(8,128)(2,1)}, u32[]{:S(2)}) copy-start(bf16[27,64,64]{2,1,0:T(8,128)(2,1)} %copy.467) | copy-start | bytes 663556
  (45 other events, 152.3 us)
Sparse Core Ops, SparseCore 0:
  727.4 26.0 reduce-scatter.3
where the time goes:
time: 870 us; the launch traced here: 861 us
  blocking collectives  516 us (59%)
  local copies, waits for them, and re-layouts  190 us (22%)
  other arithmetic  69.3 us (8%)
  starting transfers between devices  33.8 us (4%)
  matrix products  32 us (4%)
  between operations  18.3 us (2%)
    psum x1, blocking collectives, body(): weight_total, bias_total = lax.psum((weight_grad, bias_grad), 'space')  494 us
    concatenate x12, local copies, waits for them, and re-layouts, gathered_columns(): jnp.concatenate([window.reshape(-1, window.shape[-1]) for window in windo...  57.6 us
    gather x52, local copies, waits for them, and re-layouts, halo_block(): jnp.take(units, jnp.clip(unit_index, 0, unit_total - 1), axis=0)  48.9 us
    broadcast_in_dim x52, other arithmetic, rim_region(): return jnp.expand_dims(region, moving + 1)  35.8 us
    ppermute x8, starting transfers between devices, passed_along(): return lax.ppermute(block, axis, route)  33.8 us
    slice x12, local copies, waits for them, and re-layouts, windows(): padded[:, first:first + brick_edge, second:second + brick_edge, third:thi...  27.8 us
    dot_general x8, matrix products, convolve_per_brick(): jnp.dot(gathered_columns(brick_block, brick_edge), stacked_kernel, prefer...  20.7 us
  transfers between devices with their start and end apart: 9, of which 1 were waited for; matrix products, arithmetic and copies ran while one was open for 17% of the time, Pallas kernels for 0%

commit v1 on v0

v1 whole, which is shorter than its diff:
```python
import jax
import jax.numpy as jnp
from jax import lax
from jax.experimental import pallas as pl
from jax.experimental.pallas import tpu as pltpu
from jax.sharding import PartitionSpec as P

F32 = jnp.float32
BF16 = jnp.bfloat16
MESH = pl.DeviceIdType.MESH
SPACE = 128
DP = 4
GROUP = 8
ZS = 16
COLS = 5
ROWS = 256
LANES = 512
WIDE = 2304
TILES = 14
PACKED = 224
PADDED = 256
PIECE = 32
NEAR = (1, 2, SPACE - 1, SPACE - 2)
XY_LINKS = ((0, 1), (2, 3), (6, 7), (8, 9))


def low_half(shape):
    return lax.broadcasted_iota(jnp.int32, shape, len(shape) - 1) < 64


def near_column(step):
    return {1: 3, 2: 4, SPACE - 1: 1, SPACE - 2: 0}[step]


def swap_halves(v):
    return pltpu.roll(v, 64, axis=v.ndim - 1)


def keep(src, flat, sides, q, values):
    src[q, 0:8] = jnp.zeros((8, 8, 128), F32)
    src[q, 8:40] = values.reshape(32, 8, 128)
    flat[q] = values
    for y in range(2):
        sides[5 * y, :, 128 * q : 128 * q + 128] = jnp.zeros((8, 128), F32)
        for b in range(4):
            rows = pl.ds(64 * b + 7 * y, 8, stride=8)
            sides[5 * y + b + 1, :, 128 * q : 128 * q + 128] = flat[q, rows, :]


def pack_faces(src, sides, snd, out_xy, out_z):
    def slot_of(column, link):
        return ((snd[column, link] + 6) * 43) >> 8

    def plane(column, link):
        slot = slot_of(column, link)
        face = link % 6
        if face >= 2:
            return sides[5 * (face - 2) + slot]
        return jnp.concatenate([src[q, slot * 8 + 7 * face] for q in range(4)], axis=1)

    low = low_half((64, 128))
    for column in range(COLS):
        for q, pair in enumerate(XY_LINKS):
            both = jnp.concatenate([plane(column, link) for link in pair], axis=0)
            out_xy[column, 16 * q : 16 * q + 16, :] = both.astype(BF16)
        for h in range(2):
            first = src[0, pl.ds(slot_of(column, 4 + 6 * h) * 8, 8)].reshape(64, 128)
            last = src[3, pl.ds(slot_of(column, 5 + 6 * h) * 8, 8)].reshape(64, 128)
            both = jnp.where(low, first, last)
            out_z[column, 64 * h : 64 * h + 64, :] = both.astype(BF16)


def face_copies(send_xy, send_z, recv_xy, recv_z, sems):
    me = lax.axis_index("space")
    copies = []
    for n, step in enumerate(NEAR):
        column = near_column(step)
        peer = lax.rem(me + step, SPACE)
        for m, (src, dst) in enumerate(((send_xy, recv_xy), (send_z, recv_z))):
            copies.append(
                pltpu.make_async_remote_copy(
                    src_ref=src.at[column],
                    dst_ref=dst.at[column],
                    send_sem=sems.at[0, 2 * n + m],
                    recv_sem=sems.at[1, 2 * n + m],
                    device_id={"space": peer},
                    device_id_type=MESH,
                )
            )
    return copies


def own_faces(send_xy, send_z, recv_xy, recv_z):
    recv_xy[2] = send_xy[2]
    recv_z[2] = send_z[2]


def first_kernel(
    feat, occ, cnt, snd, w, bias,
    units_xy, units_z, masked, mask, wall,
    ms, flat, sides, send_xy, send_z, wsend, sems, wsems,
):
    me, part = lax.axis_index("space"), lax.axis_index("dp")
    barrier = pltpu.get_barrier_semaphore()
    for step in NEAR:
        pl.semaphore_signal(
            barrier, inc=1, device_id={"space": lax.rem(me + step, SPACE)}, device_id_type=MESH
        )
    for d in range(1, DP):
        pl.semaphore_signal(
            barrier, inc=1, device_id={"dp": lax.rem(part + d, DP)}, device_id_type=MESH
        )

    for m in range(TILES):
        top = w[32 * m : 32 * m + 16, :].astype(F32)
        if m < TILES - 1:
            other = w[32 * m + 16 : 32 * m + 32, :].astype(F32)
        else:
            row = jnp.concatenate([bias[...].astype(F32), jnp.zeros((1, 48), F32)], axis=1)
            first = lax.broadcasted_iota(jnp.int32, (16, 64), 0) == 0
            other = jnp.where(first, jnp.broadcast_to(row, (16, 64)), 0.0)
        wsend[16 * m : 16 * m + 16, :] = jnp.concatenate([top, other], axis=1).astype(BF16)

    place = lax.broadcasted_iota(jnp.int32, (64, LANES), 1)
    owner = (place >> 3) == lax.broadcasted_iota(jnp.int32, (64, LANES), 0)
    spread = []
    for b in range(4):
        live = jnp.minimum(jnp.maximum(cnt[0, 0] - b, 0), 1)
        row = (occ[b : b + 1, :] * live).astype(F32)
        spread.append(jnp.where(owner, jnp.broadcast_to(row, (64, LANES)), 0.0))
    fold = lax.broadcasted_iota(jnp.int32, (LANES, 128), 0) & 7
    fold = (fold == lax.broadcasted_iota(jnp.int32, (LANES, 128), 1)).astype(F32).astype(BF16)
    by_z = jnp.dot(jnp.concatenate(spread, axis=0).astype(BF16), fold, preferred_element_type=F32)
    widen = lax.broadcasted_iota(jnp.int32, (128, LANES), 1) >> 6
    widen = (widen == lax.broadcasted_iota(jnp.int32, (128, LANES), 0)).astype(F32).astype(BF16)
    active = jnp.dot(by_z.astype(BF16), widen, preferred_element_type=F32)
    mask[...] = active.astype(BF16)
    values = feat[...].astype(F32) * active
    for q in range(4):
        keep(ms, flat, sides, q, values[:, 128 * q : 128 * q + 128])
    masked[...] = values.astype(BF16)
    pack_faces(ms, sides, snd, send_xy, send_z)

    pl.semaphore_wait(barrier, len(NEAR) + DP - 1)
    copies = face_copies(send_xy, send_z, units_xy, units_z, sems)
    for d in range(1, DP):
        copies.append(
            pltpu.make_async_remote_copy(
                src_ref=wsend,
                dst_ref=wall.at[part],
                send_sem=wsems.at[0, d],
                recv_sem=wsems.at[1, d],
                device_id={"dp": lax.rem(part + d, DP)},
                device_id_type=MESH,
            )
        )
    for copy in copies:
        copy.start()
    wall[part] = wsend[...]
    own_faces(send_xy, send_z, units_xy, units_z)
    for copy in copies:
        copy.wait()


def read_units(units_xy, units_z, u_xy, u_z):
    for column in range(COLS):
        planes = units_xy[column].astype(F32)
        u_xy[8 * column + 8 : 8 * column + 16] = planes.reshape(8, 8, LANES)
        planes = units_z[column].astype(F32)
        u_z[2 * column + 2 : 2 * column + 4] = planes.reshape(2, 64, 128)


def build_columns(src, nbr, u_xy, u_z, stage, columns):
    low = low_half((8, 128))
    low_row = low_half((1, 128))
    depth = lax.broadcasted_iota(jnp.int32, (8, 640), 0)

    def one_brick(b, carry):
        where_of = {}
        for first in range(3):
            for second in range(3):
                for third in range(3):
                    o = (first - 1, second - 1, third - 1)
                    k = first * 9 + second * 3 + third
                    if k == 13:
                        continue
                    n = nbr[b, k if k < 13 else k - 1] + 12
                    column = (n * 171) >> 11
                    upper = (n - column * 12 + 2) >> 3
                    d = 0 if o[0] else 1 if o[1] else 2
                    face = 2 * d + (0 if o[d] == 1 else 1)
                    if d < 2:
                        where_of[o] = column * 8 + face + 4 * upper
                    else:
                        where_of[o] = column * 2 + upper

        def expand(c):
            t = [c[:, 128 * i : 128 * i + 128] for i in range(5)]
            return jnp.concatenate(
                [
                    t[0], jnp.where(low, t[1], t[4]),
                    t[1], jnp.where(low, t[2], t[0]),
                    t[2], jnp.where(low, t[3], t[1]),
                    t[3], jnp.where(low, t[4], t[2]),
                ],
                axis=1,
            )

        def side_row(ox, oy, row):
            rows = slice(row, row + 1)
            middle = u_xy[where_of[ox, oy, 0], rows, :]
            after = u_xy[where_of[ox, oy, 1], rows, 0:128]
            before = u_xy[where_of[ox, oy, -1], rows, 384:512]
            return jnp.concatenate([middle, jnp.where(low_row, after, before)], axis=1)

        for xx in range(10):
            if 1 <= xx <= 8:
                here = jnp.concatenate([src[q, b * 8 + 7 + xx] for q in range(4)], axis=1)
                rows = slice(8 * xx - 8, 8 * xx)
                after = u_z[where_of[0, 0, 1], rows, :]
                before = u_z[where_of[0, 0, -1], rows, :]
                lower, upper = side_row(0, -1, xx - 1), side_row(0, 1, xx - 1)
            else:
                ox = -1 if xx == 0 else 1
                here = u_xy[where_of[ox, 0, 0]]
                after = u_xy[where_of[ox, 0, 1], :, 0:128]
                before = u_xy[where_of[ox, 0, -1], :, 384:512]
                lower, upper = side_row(ox, -1, 7), side_row(ox, 1, 0)
            c = jnp.concatenate([here, jnp.where(low, after, before)], axis=1)
            down = jnp.where(depth == 0, jnp.broadcast_to(lower, (8, 640)), pltpu.roll(c, 1, axis=0))
            up = jnp.where(depth == 7, jnp.broadcast_to(upper, (8, 640)), pltpu.roll(c, 7, axis=0))
            for e, tile in enumerate((down, c, up)):
                stage[e, 8 * xx : 8 * xx + 8, :] = expand(tile)
        for a in range(3):
            for e in range(3):
                t = 3 * a + e
                for p in range(4):
                    rows = pl.ds(pl.multiple_of(b * 64, 64) + 256 * p, 64)
                    columns[rows, 256 * t : 256 * t + 256] = stage[
                        e, 8 * a : 8 * a + 64, 256 * p : 256 * p + 256
                    ].astype(BF16)
        return carry

    lax.fori_loop(0, 4, one_brick, 0)


def build_bands(wall, both, forward, backward):
    low = low_half((16, 128))
    for i in range(DP):
        for m in range(TILES):
            tile = wall[i, 16 * m : 16 * m + 16, :].astype(F32)
            turned = swap_halves(tile)
            row = 16 * (27 * i + 2 * m)
            both[row : row + 16, :] = jnp.where(low, tile, turned)
            if m < TILES - 1:
                both[row + 16 : row + 32, :] = jnp.where(low, turned, tile)
    low = low_half((64, 128))
    for t in range(9):
        w0, w1, w2 = (both[64 * (3 * t + f) : 64 * (3 * t + f) + 64, :] for f in range(3))
        parts = [
            jnp.where(low, w1, w0),
            jnp.where(low, w2, w1),
            jnp.where(low, 0.0, w2),
            jnp.where(low, w0, 0.0),
        ]
        for n, part in enumerate(parts):
            part = part.astype(BF16)
            row = 256 * t + 64 * n
            forward[row : row + 64, :] = part
            lane = 256 * (8 - t) + 128 * (n // 2)
            row = 64 * (n % 2)
            backward[row : row + 64, lane : lane + 128] = part


def whole_bias(wall):
    lane = lax.broadcasted_iota(jnp.int32, (16, 128), 1)
    total = jnp.zeros((16, 128), F32)
    for i in range(DP):
        tile = wall[i, PACKED - 16 : PACKED, :].astype(F32)
        tile = jnp.where((lane >= 64) & (lane < 80), tile, 0.0)
        total += pltpu.roll(tile, 64 + 16 * i, axis=1)
        total += pltpu.roll(tile, 16 * i, axis=1) if i else tile
    return total[0:1, :]


def second_kernel(
    masked, mask, cot, units_xy, units_z, wall, nbr, snd,
    block_out, grad_in, gw, gb,
    src, u_xy, u_z, stage, columns, both, forward, backward,
    grad, flat, sides, send_xy, send_z, recv_xy, recv_z, turned,
    sums, packed, dp_recv, dp_sum, y_recv, z_recv, full,
    sems, dp_sems, y_sems, z_sems, ag_sems,
):
    me, part = lax.axis_index("space"), lax.axis_index("dp")
    zed, spot = me // GROUP, lax.rem(me, GROUP)
    barrier = pltpu.get_barrier_semaphore()

    def in_group(d):
        return {"space": zed * GROUP + lax.rem(spot + d, GROUP)}

    def along_z(d):
        return {"space": lax.rem(zed + d, ZS) * GROUP + spot}

    def along_dp(d):
        return {"dp": lax.rem(part + d, DP)}

    peers = [along_z(d) for d in range(1, ZS)]
    peers += [{"space": lax.rem(me + step, SPACE)} for step in NEAR]
    peers += [along_dp(d) for d in range(1, DP)] + [in_group(d) for d in range(1, GROUP)]
    for peer in peers:
        pl.semaphore_signal(barrier, inc=1, device_id=peer, device_id_type=MESH)

    u_xy[0:8] = jnp.zeros((8, 8, LANES), F32)
    u_z[0:2] = jnp.zeros((2, 64, 128), F32)
    build_bands(wall, both, forward, backward)
    read_units(units_xy, units_z, u_xy, u_z)
    for q in range(4):
        values = masked[:, 128 * q : 128 * q + 128].astype(F32)
        src[q, 8:40] = values.reshape(32, 8, 128)
    build_columns(src, nbr, u_xy, u_z, stage, columns)

    bias = whole_bias(wall)
    bias_sum = jnp.zeros((1, 128), F32)
    for p in range(4):
        lanes = slice(128 * p, 128 * p + 128)
        pre = jnp.dot(
            columns[256 * p : 256 * p + 256, :], forward[...], preferred_element_type=F32
        )
        pre = pre + bias
        sig = jax.nn.sigmoid(pre)
        on = mask[:, lanes].astype(F32)
        block_out[:, lanes] = (pre * sig * on).astype(BF16)
        g = cot[:, lanes].astype(F32) * sig * (1.0 + pre * (1.0 - sig)) * on
        g = g.astype(BF16).astype(F32)
        keep(grad, flat, sides, p, g)
        turned[:, 256 * p : 256 * p + 256] = g.T.astype(BF16)
        bias_sum += jnp.sum(g, axis=0, keepdims=True)
    pack_faces(grad, sides, snd, send_xy, send_z)

    pl.semaphore_wait(barrier, len(peers))
    face = face_copies(send_xy, send_z, recv_xy, recv_z, sems)
    for copy in face:
        copy.start()
    own_faces(send_xy, send_z, recv_xy, recv_z)

    for t in range(9):
        r = jnp.dot(
            turned[...], columns[:, 256 * t : 256 * t + 256], preferred_element_type=F32
        ).T
        r0, r1, r2, r3 = (r[64 * n : 64 * n + 64, :] for n in range(4))
        row = 192 * t
        sums[row : row + 64, :] = r3 + swap_halves(r0)
        sums[row + 64 : row + 128, :] = r0 + swap_halves(r1)
        sums[row + 128 : row + 192, :] = r1 + swap_halves(r2)
    low = low_half((16, 128))
    top_row = lax.broadcasted_iota(jnp.int32, (16, 128), 0) == 0
    bias_sum = bias_sum + swap_halves(bias_sum)
    bias_tile = jnp.where(top_row, jnp.broadcast_to(bias_sum, (16, 128)), 0.0)
    for i in range(DP):
        for m in range(TILES):
            row = 16 * (27 * i + 2 * m)
            if m < TILES - 1:
                other = swap_halves(sums[row + 16 : row + 32, :])
            else:
                other = bias_tile
            tile = jnp.where(low, sums[row : row + 16, :], other)
            packed[i, 16 * m : 16 * m + 16, :] = tile.astype(BF16)
        packed[i, PACKED:PADDED, :] = jnp.zeros((PADDED - PACKED, 128), BF16)

    dp_copies = [
        pltpu.make_async_remote_copy(
            src_ref=packed.at[lax.rem(part + d, DP)],
            dst_ref=dp_recv.at[d - 1],
            send_sem=dp_sems.at[0, d],
            recv_sem=dp_sems.at[1, d],
            device_id=along_dp(d),
            device_id_type=MESH,
        )
        for d in range(1, DP)
    ]
    for copy in dp_copies:
        copy.start()

    for copy in face:
        copy.wait()
    read_units(recv_xy, recv_z, u_xy, u_z)
    build_columns(grad, nbr, u_xy, u_z, stage, columns)

    def grad_input(p):
        lanes = slice(128 * p, 128 * p + 128)
        r = lax.dot_general(
            columns[256 * p : 256 * p + 256, :],
            backward[...],
            (((1,), (1,)), ((), ())),
            preferred_element_type=F32,
        )
        grad_in[:, lanes] = (r * mask[:, lanes].astype(F32)).astype(BF16)

    for copy in dp_copies:
        copy.wait()
    total = packed[part].astype(F32)
    for d in range(DP - 1):
        total += dp_recv[d].astype(F32)
    dp_sum[...] = total.astype(BF16)
    y_copies = [
        pltpu.make_async_remote_copy(
            src_ref=dp_sum.at[pl.ds(pl.multiple_of(lax.rem(spot + d, GROUP) * PIECE, PIECE), PIECE)],
            dst_ref=y_recv.at[d - 1],
            send_sem=y_sems.at[0, d],
            recv_sem=y_sems.at[1, d],
            device_id=in_group(d),
            device_id_type=MESH,
        )
        for d in range(1, GROUP)
    ]
    for copy in y_copies:
        copy.start()
    grad_input(0)
    grad_input(1)

    for copy in y_copies:
        copy.wait()
    mine = pl.ds(pl.multiple_of(spot * PIECE, PIECE), PIECE)
    total = dp_sum[mine, :].astype(F32)
    for d in range(GROUP - 1):
        total += y_recv[d].astype(F32)
    z_recv[zed] = total.astype(BF16)
    z_copies = [
        pltpu.make_async_remote_copy(
            src_ref=z_recv.at[zed],
            dst_ref=z_recv.at[zed],
            send_sem=z_sems.at[0, d],
            recv_sem=z_sems.at[1, d],
            device_id=along_z(d),
            device_id_type=MESH,
        )
        for d in (8, 7, 9, 6, 10, 5, 11, 4, 12, 3, 13, 2, 14, 1, 15)
    ]
    for copy in z_copies:
        copy.start()
    grad_input(2)
    grad_input(3)

    for copy in z_copies:
        copy.wait()
    total = z_recv[0].astype(F32)
    for d in range(1, ZS):
        total += z_recv[d].astype(F32)
    full[mine, :] = total.astype(BF16)
    ag_copies = [
        pltpu.make_async_remote_copy(
            src_ref=full.at[mine],
            dst_ref=full.at[mine],
            send_sem=ag_sems.at[0, d],
            recv_sem=ag_sems.at[1, d],
            device_id=in_group(d),
            device_id_type=MESH,
        )
        for d in range(1, GROUP)
    ]
    for copy in ag_copies:
        copy.start()
    for copy in ag_copies:
        copy.wait()

    for m in range(TILES):
        tile = full[16 * m : 16 * m + 16, :].astype(F32)
        other = swap_halves(tile)
        gw[32 * m : 32 * m + 16, :] = tile[:, 0:64]
        if m < TILES - 1:
            gw[32 * m + 16 : 32 * m + 32, :] = other[:, 0:64]
        else:
            picked = jnp.zeros((16, 128), F32)
            for i in range(DP):
                turn = pltpu.roll(other, 128 - 16 * i, axis=1) if i else other
                picked = jnp.where(part == i, turn, picked)
            gb[...] = picked[0:1, 0:16]


def vmem(n):
    return [pl.BlockSpec(memory_space=pltpu.VMEM)] * n


def smem(n):
    return [pl.BlockSpec(memory_space=pltpu.SMEM)] * n


def of(shape, dtype):
    return jax.ShapeDtypeStruct(shape, dtype)


def body(features, occupancy, counts, send_units, neighbours, weight, conv_bias, cotangent):
    shard_shape = features.shape
    sends = send_units[0, 0]
    units_xy, units_z, masked, mask, wall = pl.pallas_call(
        first_kernel,
        out_shape=(
            of((COLS, 64, LANES), BF16),
            of((COLS, 128, 128), BF16),
            of((ROWS, LANES), BF16),
            of((ROWS, LANES), BF16),
            of((DP, PACKED, 128), BF16),
        ),
        in_specs=vmem(2) + smem(2) + vmem(2),
        out_specs=tuple(vmem(5)),
        scratch_shapes=[
            pltpu.VMEM((4, 40, 8, 128), F32),
            pltpu.VMEM((4, ROWS, 128), F32),
            pltpu.VMEM((10, 8, LANES), F32),
            pltpu.VMEM((COLS, 64, LANES), BF16),
            pltpu.VMEM((COLS, 128, 128), BF16),
            pltpu.VMEM((PACKED, 128), BF16),
            pltpu.SemaphoreType.DMA((2, 8)),
            pltpu.SemaphoreType.DMA((2, DP)),
        ],
        compiler_params=pltpu.CompilerParams(collective_id=0, has_side_effects=True),
        name="trade_faces",
    )(
        features.reshape(ROWS, LANES), occupancy[0], counts, sends, weight, conv_bias.reshape(1, 16)
    )
    block_out, grad_in, gw, gb = pl.pallas_call(
        second_kernel,
        out_shape=(
            of((ROWS, LANES), BF16),
            of((ROWS, LANES), BF16),
            of((432, 64), F32),
            of((1, 16), F32),
        ),
        in_specs=vmem(6) + smem(2),
        out_specs=tuple(vmem(4)),
        scratch_shapes=[
            pltpu.VMEM((4, 40, 8, 128), F32),
            pltpu.VMEM((48, 8, LANES), F32),
            pltpu.VMEM((12, 64, 128), F32),
            pltpu.VMEM((3, 80, 1024), F32),
            pltpu.VMEM((1024, WIDE), BF16),
            pltpu.VMEM((1728, 128), F32),
            pltpu.VMEM((WIDE, 128), BF16),
            pltpu.VMEM((128, WIDE), BF16),
            pltpu.VMEM((4, 40, 8, 128), F32),
            pltpu.VMEM((4, ROWS, 128), F32),
            pltpu.VMEM((10, 8, LANES), F32),
            pltpu.VMEM((COLS, 64, LANES), BF16),
            pltpu.VMEM((COLS, 128, 128), BF16),
            pltpu.VMEM((COLS, 64, LANES), BF16),
            pltpu.VMEM((COLS, 128, 128), BF16),
            pltpu.VMEM((128, 1024), BF16),
            pltpu.VMEM((1728, 128), F32),
            pltpu.VMEM((DP, PADDED, 128), BF16),
            pltpu.VMEM((DP - 1, PADDED, 128), BF16),
            pltpu.VMEM((PADDED, 128), BF16),
            pltpu.VMEM((GROUP - 1, PIECE, 128), BF16),
            pltpu.VMEM((ZS, PIECE, 128), BF16),
            pltpu.VMEM((PADDED, 128), BF16),
            pltpu.SemaphoreType.DMA((2, 8)),
            pltpu.SemaphoreType.DMA((2, DP)),
            pltpu.SemaphoreType.DMA((2, GROUP)),
            pltpu.SemaphoreType.DMA((2, ZS)),
            pltpu.SemaphoreType.DMA((2, GROUP)),
        ],
        compiler_params=pltpu.CompilerParams(
            collective_id=1, has_side_effects=True, vmem_limit_bytes=60 * 1024 * 1024
        ),
        name="convolve_and_reduce",
    )(
        masked, mask, cotangent.reshape(ROWS, LANES), units_xy, units_z, wall, neighbours[0], sends
    )
    return block_out.reshape(shard_shape), grad_in.reshape(shard_shape), gw, gb.reshape(16)


def solution(mesh):
    placed = (
        P("dp", "space", None, None, None),
        P("dp", "space", None),
        P("dp", "space"),
        P("dp", "space", None, None),
        P("dp", "space", None),
        P("dp", None),
        P("dp"),
        P("dp", "space", None, None, None),
    )
    return jax.shard_map(
        body,
        mesh=mesh,
        in_specs=placed,
        out_specs=(
            P("dp", "space", None, None, None),
            P("dp", "space", None, None, None),
            P("dp", None),
            P("dp"),
        ),
        check_vma=False,
    )
```

time: 870 us -> 63.4 us (0.07); the launches traced: 861 us -> 63.1 us
  blocking collectives: 516 us -> 0 us
  local copies, waits for them, and re-layouts: 190 us -> 6.88 us
  other arithmetic: 69.3 us -> 0 us
  Pallas kernels: 0 us -> 54.9 us
  starting transfers between devices: 33.8 us -> 0 us
  matrix products: 32 us -> 0 us
  between operations: 18.3 us -> 1.31 us
    psum x1 -> x0, blocking collectives: 494 us -> none  [body(): weight_total, bias_total = lax.psum((weight_grad, bias_grad), 'space')]
    concatenate x12 -> x0, local copies, waits for them, and re-layouts: 57.6 us -> none  [gathered_columns(): jnp.concatenate([window.reshape(-1, window.shape[-1]) for window in windo...]
    pallas_call x0 -> x2, Pallas kernels: none -> 54.9 us  [the longest x1 32.3 us: body(): pl.pallas_call(second_kernel, out_shape=(of((ROWS, LANES), BF16), of((ROW...]
    gather x54 -> x0, local copies, waits for them, and re-layouts: 50.2 us -> none  [the longest x52 48.9 us: halo_block(): jnp.take(units, jnp.clip(unit_index, 0, unit_total - 1), axis=0)]
    broadcast_in_dim x52 -> x0, other arithmetic: 35.8 us -> none  [rim_region(): return jnp.expand_dims(region, moving + 1)]
    ppermute x8 -> x0, starting transfers between devices: 33.8 us -> none  [passed_along(): return lax.ppermute(block, axis, route)]
    dot_general x12 -> x0, matrix products: 32 us -> none  [the longest x8 20.7 us: convolve_per_brick(): jnp.dot(gathered_columns(brick_block, brick_edge), stacked_kernel, prefer...]
    slice x16 -> x0, local copies, waits for them, and re-layouts: 29.6 us -> none  [the longest x12 27.8 us: windows(): padded[:, first:first + brick_edge, second:second + brick_edge, third:thi...]
  transfers between devices with their start and end apart: 9 -> 0, of which waited for: 1 -> 0; matrix products, arithmetic and copies ran while one was open for 17% -> 0% of each run, Pallas kernels for 0% -> 0%
where the time goes in v1:
time: 63.4 us; the launch traced here: 63.1 us
  Pallas kernels  54.9 us (87%)
  local copies, waits for them, and re-layouts  6.88 us (11%)
  between operations  1.31 us (2%)
    pallas_call x1, Pallas kernels, body(): pl.pallas_call(second_kernel, out_shape=(of((ROWS, LANES), BF16), of((ROW...  32.3 us
    pallas_call x1, Pallas kernels, body(): pl.pallas_call(first_kernel, out_shape=(of((COLS, 64, LANES), BF16), of((...  22.6 us
    unnamed x14, local copies, waits for them, and re-layouts  6.88 us

profile of v1, /device:TPU:1, one launch (start us, length us, event | category | flops | bytes accessed | tf_op | source)
XLA Modules:
  0.0 63.1 jit_solution(18385417911887477819)
XLA Ops:
  1.3 0.0 copy-start.2
  1.3 0.7 %copy-done.2 = s32[1,1,5,12]{3,1,2,0:T(1,128)S(1)} copy-done((s32[1,1,5,12]{3,1,2,0:T(1,128)S(1)}, s32[1,1,5,12]{3,1,2,0:T(1,128)}, u32[]{:S(2)}) %copy-start.2) | copy-done | bytes 264
  2.0 0.6 copy.16
  2.6 1.6 %copy.12.w = bf16[432,64]{1,0:T(8,128)(2,1)} copy(bf16[432,64]{0,1:T(8,128)(2,1)} %param.13) | data formatting | bytes 110592 | tf_op args[5]
  4.2 22.6 %trade_faces.1 = (bf16[5,64,512]{2,1,0:T(8,128)(2,1)}, bf16[5,128,128]{2,1,0:T(8,128)(2,1)}, bf16[256,512]{1,0:T(8,128)(2,1)}, bf16[256,512]{1,0:T(8,128)(2,1)}, bf16[4,224,128]{2,1,0:T(8,128)(2,1)}) custom-call(bf16[256,512]{1,0:T(8,128)(2,1)} %bitcast.11, s32[4,512]{1,0:T(4,128)} %bitcast.17, s32[1,1]{1,0:T(1,128)S(6)} %copy.20.cnt, s32[5,12]{1,0:T(8,128)} %bitcast.15, ...), custom_call_target="tpu_custom_call" | custom-call | tf_op jit(solution)/shard_map/trade_faces/pallas_call | solution.py:495
  26.7 32.3 %convolve_and_reduce.1 = (bf16[256,512]{1,0:T(8,128)(2,1)}, bf16[256,512]{1,0:T(8,128)(2,1)}, f32[432,64]{1,0:T(8,128)}, f32[1,16]{1,0:T(1,128)}) custom-call(bf16[256,512]{1,0:T(8,128)(2,1)} %get-tuple-element.13.masked, bf16[256,512]{1,0:T(8,128)(2,1)} %get-tuple-element.14.mask, bf16[256,512]{1,0:T(8,128)(2,1)} %bitcast.14, ...), custom_call_target="tpu_custom_call" | custom-call | tf_op jit(solution)/shard_map/convolve_and_reduce/pallas_call | solution.py:521
  59.0 0.0 copy-start.1
  59.0 1.8 %copy.13 = f32[432,64]{0,1:T(8,128)} copy(f32[432,64]{1,0:T(8,128)} %get-tuple-element.24) | data formatting | bytes 221184
  60.8 0.0 copy-done.1
  60.8 0.0 copy-start
  60.8 0.7 %copy.21 = bf16[1,4,8,8,512]{4,3,2,1,0:T(8,128)(2,1)} copy(bf16[1,4,8,8,512]{4,3,2,1,0:T(8,128)(2,1)S(1)} %bitcast.13) | data formatting | bytes 524288
  61.5 0.3 copy-done
  61.8 0.0 copy-start.3
  61.8 0.7 %copy.22 = bf16[1,4,8,8,512]{4,3,2,1,0:T(8,128)(2,1)} copy(bf16[1,4,8,8,512]{4,3,2,1,0:T(8,128)(2,1)S(1)} %bitcast.12) | data formatting | bytes 524288
  62.5 0.0 copy-done.3
  62.5 0.5 copy.23
Async XLA Ops:
  1.3 0.7 %copy-start.2 = (s32[1,1,5,12]{3,1,2,0:T(1,128)S(1)}, s32[1,1,5,12]{3,1,2,0:T(1,128)}, u32[]{:S(2)}) copy-start(s32[1,1,5,12]{3,1,2,0:T(1,128)} %param.11) | copy-start | bytes 724
  59.0 1.8 %copy-start.1 = (bf16[256,512]{1,0:T(8,128)(2,1)S(1)}, bf16[256,512]{1,0:T(8,128)(2,1)}, u32[]{:S(2)}) copy-start(bf16[256,512]{1,0:T(8,128)(2,1)} %get-tuple-element.18) | copy-start | bytes 786436
  60.8 1.0 %copy-start = (bf16[256,512]{1,0:T(8,128)(2,1)S(1)}, bf16[256,512]{1,0:T(8,128)(2,1)}, u32[]{:S(2)}) copy-start(bf16[256,512]{1,0:T(8,128)(2,1)} %get-tuple-element.19) | copy-start | bytes 786436
  61.8 0.7 %copy-start.3 = (f32[1,16]{1,0:T(1,128)S(1)}, f32[1,16]{1,0:T(1,128)}, u32[]{:S(2)}) copy-start(f32[1,16]{1,0:T(1,128)} %get-tuple-element.21) | copy-start | bytes 196

commit v2 on v1

--- a/solution.py
+++ b/solution.py
@@ -21,6 +21,7 @@
 PADDED = 256
 PIECE = 32
 NEAR = (1, 2, SPACE - 1, SPACE - 2)
+RS_ORDER = [(dx, dg) for dx in (2, 1, 3, 0) for dg in (4, 5, 3, 2, 6, 7, 1, 0) if (dx, dg) != (0, 0)]
 XY_LINKS = ((0, 1), (2, 3), (6, 7), (8, 9))
 
 
@@ -49,7 +50,7 @@
 
 def pack_faces(src, sides, snd, out_xy, out_z):
     def slot_of(column, link):
-        return ((snd[column, link] + 6) * 43) >> 8
+        return ((snd[column, 0, link] + 6) * 43) >> 8
 
     def plane(column, link):
         slot = slot_of(column, link)
@@ -95,32 +96,23 @@
     recv_z[2] = send_z[2]
 
 
-def first_kernel(
-    feat, occ, cnt, snd, w, bias,
-    units_xy, units_z, masked, mask, wall,
-    ms, flat, sides, send_xy, send_z, wsend, sems, wsems,
-):
-    me, part = lax.axis_index("space"), lax.axis_index("dp")
-    barrier = pltpu.get_barrier_semaphore()
-    for step in NEAR:
-        pl.semaphore_signal(
-            barrier, inc=1, device_id={"space": lax.rem(me + step, SPACE)}, device_id_type=MESH
-        )
-    for d in range(1, DP):
-        pl.semaphore_signal(
-            barrier, inc=1, device_id={"dp": lax.rem(part + d, DP)}, device_id_type=MESH
-        )
-
-    for m in range(TILES):
-        top = w[32 * m : 32 * m + 16, :].astype(F32)
-        if m < TILES - 1:
-            other = w[32 * m + 16 : 32 * m + 32, :].astype(F32)
+def pack_weights(wt, bias, wsend):
+    row = jnp.concatenate([bias[...].astype(F32), jnp.zeros((1, 48), F32)], axis=1)
+    first = lax.broadcasted_iota(jnp.int32, (16, 64), 0) == 0
+    last = jnp.where(first, jnp.broadcast_to(row, (16, 64)), 0.0)
+    for n in range(4):
+        if n < 3:
+            tile = wt[:, 128 * n : 128 * n + 128].astype(F32)
         else:
-            row = jnp.concatenate([bias[...].astype(F32), jnp.zeros((1, 48), F32)], axis=1)
-            first = lax.broadcasted_iota(jnp.int32, (16, 64), 0) == 0
-            other = jnp.where(first, jnp.broadcast_to(row, (16, 64)), 0.0)
-        wsend[16 * m : 16 * m + 16, :] = jnp.concatenate([top, other], axis=1).astype(BF16)
-
+            tile = jnp.concatenate([wt[:, 384:432].astype(F32), jnp.zeros((64, 80), F32)], axis=1)
+        tile = tile.T
+        for m in range(4 if n < 3 else 2):
+            other = tile[32 * m + 16 : 32 * m + 32] if 4 * n + m < TILES - 1 else last
+            both = jnp.concatenate([tile[32 * m : 32 * m + 16], other], axis=1)
+            wsend[64 * n + 16 * m : 64 * n + 16 * m + 16, :] = both.astype(BF16)
+
+
+def expand_mask(occ, cnt):
     place = lax.broadcasted_iota(jnp.int32, (64, LANES), 1)
     owner = (place >> 3) == lax.broadcasted_iota(jnp.int32, (64, LANES), 0)
     spread = []
@@ -133,33 +125,7 @@
     by_z = jnp.dot(jnp.concatenate(spread, axis=0).astype(BF16), fold, preferred_element_type=F32)
     widen = lax.broadcasted_iota(jnp.int32, (128, LANES), 1) >> 6
     widen = (widen == lax.broadcasted_iota(jnp.int32, (128, LANES), 0)).astype(F32).astype(BF16)
-    active = jnp.dot(by_z.astype(BF16), widen, preferred_element_type=F32)
-    mask[...] = active.astype(BF16)
-    values = feat[...].astype(F32) * active
-    for q in range(4):
-        keep(ms, flat, sides, q, values[:, 128 * q : 128 * q + 128])
-    masked[...] = values.astype(BF16)
-    pack_faces(ms, sides, snd, send_xy, send_z)
-
-    pl.semaphore_wait(barrier, len(NEAR) + DP - 1)
-    copies = face_copies(send_xy, send_z, units_xy, units_z, sems)
-    for d in range(1, DP):
-        copies.append(
-            pltpu.make_async_remote_copy(
-                src_ref=wsend,
-                dst_ref=wall.at[part],
-                send_sem=wsems.at[0, d],
-                recv_sem=wsems.at[1, d],
-                device_id={"dp": lax.rem(part + d, DP)},
-                device_id_type=MESH,
-            )
-        )
-    for copy in copies:
-        copy.start()
-    wall[part] = wsend[...]
-    own_faces(send_xy, send_z, units_xy, units_z)
-    for copy in copies:
-        copy.wait()
+    return jnp.dot(by_z.astype(BF16), widen, preferred_element_type=F32)
 
 
 def read_units(units_xy, units_z, u_xy, u_z):
@@ -283,13 +249,14 @@
     return total[0:1, :]
 
 
-def second_kernel(
-    masked, mask, cot, units_xy, units_z, wall, nbr, snd,
-    block_out, grad_in, gw, gb,
+def main_kernel(
+    cnt, feat, occ, wt, bias, cot, snd_in, nbr_in,
+    block_out, grad_in, full,
+    snd, nbr, feat_v, occ_v, wt_v, bias_v, cot_v, mask, wsend, wall,
     src, u_xy, u_z, stage, columns, both, forward, backward,
-    grad, flat, sides, send_xy, send_z, recv_xy, recv_z, turned,
-    sums, packed, dp_recv, dp_sum, y_recv, z_recv, full,
-    sems, dp_sems, y_sems, z_sems, ag_sems,
+    flat, sides, send_xy, send_z, recv_xy, recv_z, send_gxy, send_gz, recv_gxy, recv_gz, turned,
+    sums, packed, rs_recv, z_recv,
+    in_sems, sems, gsems, wsems, rs_sems, z_sems, ag_sems, ready,
 ):
     me, part = lax.axis_index("space"), lax.axis_index("dp")
     zed, spot = me // GROUP, lax.rem(me, GROUP)
@@ -304,44 +271,96 @@
     def along_dp(d):
         return {"dp": lax.rem(part + d, DP)}
 
-    peers = [along_z(d) for d in range(1, ZS)]
-    peers += [{"space": lax.rem(me + step, SPACE)} for step in NEAR]
-    peers += [along_dp(d) for d in range(1, DP)] + [in_group(d) for d in range(1, GROUP)]
-    for peer in peers:
-        pl.semaphore_signal(barrier, inc=1, device_id=peer, device_id_type=MESH)
-
+    def tell(sem, peers):
+        for peer in peers:
+            pl.semaphore_signal(sem, inc=1, device_id=peer, device_id_type=MESH)
+
+    across = [along_dp(d) for d in range(1, DP)]
+    beside = [along_z(1), along_z(ZS - 1)]
+    near = [{"space": lax.rem(me + step, SPACE)} for step in NEAR]
+    near += across + beside + [in_group(d) for d in range(1, GROUP)]
+    tell(barrier, near)
+    loads = [
+        pltpu.make_async_copy(far, here, in_sems.at[n])
+        for n, (far, here) in enumerate(
+            (
+                (occ, occ_v), (feat, feat_v), (wt, wt_v), (bias, bias_v), (cot, cot_v),
+                (snd_in, snd), (nbr_in, nbr),
+            )
+        )
+    ]
+    for load in loads:
+        load.start()
+
+    loads[0].wait()
+    active = expand_mask(occ_v, cnt)
+    mask[...] = active.astype(BF16)
+    loads[1].wait()
+    values = feat_v[...].astype(F32) * active
+    for q in range(4):
+        keep(src, flat, sides, q, values[:, 128 * q : 128 * q + 128])
+    loads[5].wait()
+    pack_faces(src, sides, snd, send_xy, send_z)
+    loads[2].wait()
+    loads[3].wait()
+    pack_weights(wt_v, bias_v, wsend)
+
+    pl.semaphore_wait(barrier, len(near))
+    copies = face_copies(send_xy, send_z, recv_xy, recv_z, sems)
+    shares = [
+        pltpu.make_async_remote_copy(
+            src_ref=wsend,
+            dst_ref=wall.at[part],
+            send_sem=wsems.at[0, d],
+            recv_sem=wsems.at[1, d],
+            device_id=along_dp(d),
+            device_id_type=MESH,
+        )
+        for d in range(1, DP)
+    ]
+    for copy in copies + shares:
+        copy.start()
+    tell(ready.at[0], across + beside)
+    wall[part] = wsend[...]
+    own_faces(send_xy, send_z, recv_xy, recv_z)
     u_xy[0:8] = jnp.zeros((8, 8, LANES), F32)
     u_z[0:2] = jnp.zeros((2, 64, 128), F32)
+    for copy in shares:
+        copy.wait()
     build_bands(wall, both, forward, backward)
-    read_units(units_xy, units_z, u_xy, u_z)
-    for q in range(4):
-        values = masked[:, 128 * q : 128 * q + 128].astype(F32)
-        src[q, 8:40] = values.reshape(32, 8, 128)
+    bias_row = whole_bias(wall)
+    for copy in copies:
+        copy.wait()
+    pl.semaphore_wait(ready.at[0], len(across) + len(beside))
+    tell(ready.at[1], [along_z(2), along_z(ZS - 2)])
+
+    loads[6].wait()
+    read_units(recv_xy, recv_z, u_xy, u_z)
     build_columns(src, nbr, u_xy, u_z, stage, columns)
-
-    bias = whole_bias(wall)
+    loads[4].wait()
     bias_sum = jnp.zeros((1, 128), F32)
     for p in range(4):
         lanes = slice(128 * p, 128 * p + 128)
         pre = jnp.dot(
             columns[256 * p : 256 * p + 256, :], forward[...], preferred_element_type=F32
         )
-        pre = pre + bias
+        pre = pre + bias_row
         sig = jax.nn.sigmoid(pre)
         on = mask[:, lanes].astype(F32)
         block_out[:, lanes] = (pre * sig * on).astype(BF16)
-        g = cot[:, lanes].astype(F32) * sig * (1.0 + pre * (1.0 - sig)) * on
+        g = cot_v[:, lanes].astype(F32) * sig * (1.0 + pre * (1.0 - sig)) * on
         g = g.astype(BF16).astype(F32)
-        keep(grad, flat, sides, p, g)
+        keep(src, flat, sides, p, g)
         turned[:, 256 * p : 256 * p + 256] = g.T.astype(BF16)
         bias_sum += jnp.sum(g, axis=0, keepdims=True)
-    pack_faces(grad, sides, snd, send_xy, send_z)
-
-    pl.semaphore_wait(barrier, len(peers))
-    face = face_copies(send_xy, send_z, recv_xy, recv_z, sems)
+    pack_faces(src, sides, snd, send_gxy, send_gz)
+
+    face = face_copies(send_gxy, send_gz, recv_gxy, recv_gz, gsems)
     for copy in face:
         copy.start()
-    own_faces(send_xy, send_z, recv_xy, recv_z)
+    own_faces(send_gxy, send_gz, recv_gxy, recv_gz)
+    pl.semaphore_wait(ready.at[1], 2)
+    tell(ready.at[2], [along_z(4), along_z(ZS - 4)])
 
     for t in range(9):
         r = jnp.dot(
@@ -367,24 +386,27 @@
             packed[i, 16 * m : 16 * m + 16, :] = tile.astype(BF16)
         packed[i, PACKED:PADDED, :] = jnp.zeros((PADDED - PACKED, 128), BF16)
 
-    dp_copies = [
-        pltpu.make_async_remote_copy(
-            src_ref=packed.at[lax.rem(part + d, DP)],
-            dst_ref=dp_recv.at[d - 1],
-            send_sem=dp_sems.at[0, d],
-            recv_sem=dp_sems.at[1, d],
-            device_id=along_dp(d),
-            device_id_type=MESH,
-        )
-        for d in range(1, DP)
-    ]
-    for copy in dp_copies:
+    rs_copies = []
+    for dx, dg in RS_ORDER:
+        to = lax.rem(part + dx, DP), lax.rem(spot + dg, GROUP)
+        at = 8 * dx + dg
+        rs_copies.append(
+            pltpu.make_async_remote_copy(
+                src_ref=packed.at[to[0], pl.ds(pl.multiple_of(to[1] * PIECE, PIECE), PIECE)],
+                dst_ref=rs_recv.at[at],
+                send_sem=rs_sems.at[0, at],
+                recv_sem=rs_sems.at[1, at],
+                device_id={"space": zed * GROUP + to[1], "dp": to[0]},
+                device_id_type=MESH,
+            )
+        )
+    for copy in rs_copies:
         copy.start()
 
     for copy in face:
         copy.wait()
-    read_units(recv_xy, recv_z, u_xy, u_z)
-    build_columns(grad, nbr, u_xy, u_z, stage, columns)
+    read_units(recv_gxy, recv_gz, u_xy, u_z)
+    build_columns(src, nbr, u_xy, u_z, stage, columns)
 
     def grad_input(p):
         lanes = slice(128 * p, 128 * p + 128)
@@ -396,35 +418,14 @@
         )
         grad_in[:, lanes] = (r * mask[:, lanes].astype(F32)).astype(BF16)
 
-    for copy in dp_copies:
-        copy.wait()
-    total = packed[part].astype(F32)
-    for d in range(DP - 1):
-        total += dp_recv[d].astype(F32)
-    dp_sum[...] = total.astype(BF16)
-    y_copies = [
-        pltpu.make_async_remote_copy(
-            src_ref=dp_sum.at[pl.ds(pl.multiple_of(lax.rem(spot + d, GROUP) * PIECE, PIECE), PIECE)],
-            dst_ref=y_recv.at[d - 1],
-            send_sem=y_sems.at[0, d],
-            recv_sem=y_sems.at[1, d],
-            device_id=in_group(d),
-            device_id_type=MESH,
-        )
-        for d in range(1, GROUP)
-    ]
-    for copy in y_copies:
-        copy.start()
-    grad_input(0)
-    grad_input(1)
-
-    for copy in y_copies:
+    for copy in rs_copies:
         copy.wait()
     mine = pl.ds(pl.multiple_of(spot * PIECE, PIECE), PIECE)
-    total = dp_sum[mine, :].astype(F32)
-    for d in range(GROUP - 1):
-        total += y_recv[d].astype(F32)
+    total = packed[part, mine, :].astype(F32)
+    for at in range(1, DP * GROUP):
+        total += rs_recv[at].astype(F32)
     z_recv[zed] = total.astype(BF16)
+    pl.semaphore_wait(ready.at[2], 2)
     z_copies = [
         pltpu.make_async_remote_copy(
             src_ref=z_recv.at[zed],
@@ -438,8 +439,8 @@
     ]
     for copy in z_copies:
         copy.start()
-    grad_input(2)
-    grad_input(3)
+    for p in range(4):
+        grad_input(p)
 
     for copy in z_copies:
         copy.wait()
@@ -463,18 +464,28 @@
     for copy in ag_copies:
         copy.wait()
 
+
+def last_kernel(block_in, grad_v, full, block_out, grad_out, gw, gb, rows):
+    part = lax.axis_index("dp")
+    block_out[...] = block_in[...]
+    grad_out[...] = grad_v[...]
     for m in range(TILES):
         tile = full[16 * m : 16 * m + 16, :].astype(F32)
         other = swap_halves(tile)
-        gw[32 * m : 32 * m + 16, :] = tile[:, 0:64]
-        if m < TILES - 1:
-            gw[32 * m + 16 : 32 * m + 32, :] = other[:, 0:64]
-        else:
+        rows[32 * m : 32 * m + 16, :] = tile
+        rows[32 * m + 16 : 32 * m + 32, :] = other
+        if m == TILES - 1:
             picked = jnp.zeros((16, 128), F32)
             for i in range(DP):
                 turn = pltpu.roll(other, 128 - 16 * i, axis=1) if i else other
                 picked = jnp.where(part == i, turn, picked)
             gb[...] = picked[0:1, 0:16]
+    for n in range(4):
+        tile = rows[128 * n : 128 * n + 128, :].T[0:64, :]
+        if n < 3:
+            gw[:, 128 * n : 128 * n + 128] = tile
+        else:
+            gw[:, 384:432] = tile[:, 0:48]
 
 
 def vmem(n):
@@ -491,44 +502,23 @@
 
 def body(features, occupancy, counts, send_units, neighbours, weight, conv_bias, cotangent):
     shard_shape = features.shape
-    sends = send_units[0, 0]
-    units_xy, units_z, masked, mask, wall = pl.pallas_call(
-        first_kernel,
-        out_shape=(
-            of((COLS, 64, LANES), BF16),
-            of((COLS, 128, 128), BF16),
-            of((ROWS, LANES), BF16),
-            of((ROWS, LANES), BF16),
-            of((DP, PACKED, 128), BF16),
-        ),
-        in_specs=vmem(2) + smem(2) + vmem(2),
-        out_specs=tuple(vmem(5)),
+    sends = send_units.transpose(0, 2, 1, 3).reshape(COLS, 1, 12)
+    block_out, grad_in, full = pl.pallas_call(
+        main_kernel,
+        out_shape=(of((ROWS, LANES), BF16), of((ROWS, LANES), BF16), of((PADDED, 128), BF16)),
+        in_specs=smem(1) + [pl.BlockSpec(memory_space=pltpu.HBM)] * 7,
+        out_specs=tuple(vmem(3)),
         scratch_shapes=[
-            pltpu.VMEM((4, 40, 8, 128), F32),
-            pltpu.VMEM((4, ROWS, 128), F32),
-            pltpu.VMEM((10, 8, LANES), F32),
-            pltpu.VMEM((COLS, 64, LANES), BF16),
-            pltpu.VMEM((COLS, 128, 128), BF16),
+            pltpu.SMEM((COLS, 1, 12), jnp.int32),
+            pltpu.SMEM((4, 26), jnp.int32),
+            pltpu.VMEM((ROWS, LANES), BF16),
+            pltpu.VMEM((4, LANES), jnp.int32),
+            pltpu.VMEM((64, 432), BF16),
+            pltpu.VMEM((1, 16), BF16),
+            pltpu.VMEM((ROWS, LANES), BF16),
+            pltpu.VMEM((ROWS, LANES), BF16),
             pltpu.VMEM((PACKED, 128), BF16),
-            pltpu.SemaphoreType.DMA((2, 8)),
-            pltpu.SemaphoreType.DMA((2, DP)),
-        ],
-        compiler_params=pltpu.CompilerParams(collective_id=0, has_side_effects=True),
-        name="trade_faces",
-    )(
-        features.reshape(ROWS, LANES), occupancy[0], counts, sends, weight, conv_bias.reshape(1, 16)
-    )
-    block_out, grad_in, gw, gb = pl.pallas_call(
-        second_kernel,
-        out_shape=(
-            of((ROWS, LANES), BF16),
-            of((ROWS, LANES), BF16),
-            of((432, 64), F32),
-            of((1, 16), F32),
-        ),
-        in_specs=vmem(6) + smem(2),
-        out_specs=tuple(vmem(4)),
-        scratch_shapes=[
+            pltpu.VMEM((DP, PACKED, 128), BF16),
             pltpu.VMEM((4, 40, 8, 128), F32),
             pltpu.VMEM((48, 8, LANES), F32),
             pltpu.VMEM((12, 64, 128), F32),
@@ -537,35 +527,54 @@
             pltpu.VMEM((1728, 128), F32),
             pltpu.VMEM((WIDE, 128), BF16),
             pltpu.VMEM((128, WIDE), BF16),
-            pltpu.VMEM((4, 40, 8, 128), F32),
             pltpu.VMEM((4, ROWS, 128), F32),
             pltpu.VMEM((10, 8, LANES), F32),
-            pltpu.VMEM((COLS, 64, LANES), BF16),
-            pltpu.VMEM((COLS, 128, 128), BF16),
-            pltpu.VMEM((COLS, 64, LANES), BF16),
-            pltpu.VMEM((COLS, 128, 128), BF16),
+        ]
+        + [pltpu.VMEM((COLS, 64, LANES), BF16), pltpu.VMEM((COLS, 128, 128), BF16)] * 4
+        + [
             pltpu.VMEM((128, 1024), BF16),
             pltpu.VMEM((1728, 128), F32),
             pltpu.VMEM((DP, PADDED, 128), BF16),
-            pltpu.VMEM((DP - 1, PADDED, 128), BF16),
-            pltpu.VMEM((PADDED, 128), BF16),
-            pltpu.VMEM((GROUP - 1, PIECE, 128), BF16),
+            pltpu.VMEM((DP * GROUP, PIECE, 128), BF16),
             pltpu.VMEM((ZS, PIECE, 128), BF16),
-            pltpu.VMEM((PADDED, 128), BF16),
+            pltpu.SemaphoreType.DMA((7,)),
+            pltpu.SemaphoreType.DMA((2, 8)),
             pltpu.SemaphoreType.DMA((2, 8)),
             pltpu.SemaphoreType.DMA((2, DP)),
-            pltpu.SemaphoreType.DMA((2, GROUP)),
+            pltpu.SemaphoreType.DMA((2, DP * GROUP)),
             pltpu.SemaphoreType.DMA((2, ZS)),
             pltpu.SemaphoreType.DMA((2, GROUP)),
+            pltpu.SemaphoreType.REGULAR((3,)),
         ],
         compiler_params=pltpu.CompilerParams(
-            collective_id=1, has_side_effects=True, vmem_limit_bytes=60 * 1024 * 1024
+            collective_id=0, has_side_effects=True, vmem_limit_bytes=24 * 1024 * 1024
         ),
-        name="convolve_and_reduce",
+        name="main",
     )(
-        masked, mask, cotangent.reshape(ROWS, LANES), units_xy, units_z, wall, neighbours[0], sends
+        counts,
+        *(
+            pltpu.with_memory_space_constraint(x, pltpu.HBM)
+            for x in (
+                features.reshape(ROWS, LANES), occupancy[0], weight.T, conv_bias.reshape(1, 16),
+                cotangent.reshape(ROWS, LANES), sends, neighbours[0],
+            )
+        )
     )
-    return block_out.reshape(shard_shape), grad_in.reshape(shard_shape), gw, gb.reshape(16)
+    block_out, grad_in, gw, gb = pl.pallas_call(
+        last_kernel,
+        out_shape=(
+            of((ROWS, LANES), BF16),
+            of((ROWS, LANES), BF16),
+            of((64, 432), F32),
+            of((1, 16), F32),
+        ),
+        in_specs=vmem(3),
+        out_specs=tuple(vmem(4)),
+        scratch_shapes=[pltpu.VMEM((512, 128), F32)],
+        compiler_params=pltpu.CompilerParams(vmem_limit_bytes=8 * 1024 * 1024),
+        name="finish",
+    )(block_out, grad_in, full)
+    return block_out.reshape(shard_shape), grad_in.reshape(shard_shape), gw.T, gb.reshape(16)
 
 
 def solution(mesh):

time: 63.4 us -> 48.8 us (0.77)
  Pallas kernels: 54.9 us -> 47.4 us
  local copies, waits for them, and re-layouts: 6.88 us -> 0 us
    pallas_call x2, Pallas kernels: 54.9 us -> 47.4 us  [the longest x1 46.4 us: body(): pl.pallas_call(main_kernel, out_shape=(of((ROWS, LANES), BF16), of((ROWS,...]
    unnamed x14 -> x0, local copies, waits for them, and re-layouts: 6.88 us -> none
where the time goes in v2:
time: 48.8 us; the launch traced here: 48.6 us
  Pallas kernels  47.4 us (97%)
  between operations  1.29 us (3%)
    pallas_call x1, Pallas kernels, body(): pl.pallas_call(main_kernel, out_shape=(of((ROWS, LANES), BF16), of((ROWS,...  46.4 us
    pallas_call x1, Pallas kernels, body(): pl.pallas_call(last_kernel, out_shape=(of((ROWS, LANES), BF16), of((ROWS,...  0.99 us

profile of v2, /device:TPU:1, one launch (start us, length us, event | category | flops | bytes accessed | tf_op | source)
XLA Modules:
  0.0 48.6 jit_solution(6345978575491780834)
XLA Ops:
  1.3 46.4 %main.1 = (bf16[256,512]{1,0:T(8,128)(2,1)S(1)}, bf16[256,512]{1,0:T(8,128)(2,1)S(1)}, bf16[256,128]{1,0:T(8,128)(2,1)S(1)}) custom-call(s32[1,1]{1,0:T(1,128)S(6)} %copy.12.cnt, bf16[256,512]{1,0:T(8,128)(2,1)} %bitcast.11, s32[4,512]{1,0:T(4,128)} %bitcast.14, bf16[64,432]{1,0:T(8,128)(2,1)} %bitcast.13, bf16[1,16]{1,0:T(2,128)(2,1)} %bitcast.17, ...), custom_call_target="tpu_custom_call" | custom-call | tf_op jit(solution)/shard_map/main/pallas_call | solution.py:506
  47.6 1.0 %finish.1 = (bf16[256,512]{1,0:T(8,128)(2,1)}, bf16[256,512]{1,0:T(8,128)(2,1)}, f32[64,432]{1,0:T(8,128)}, f32[1,16]{1,0:T(1,128)}) custom-call(bf16[256,512]{1,0:T(8,128)(2,1)S(1)} %get-tuple-element.11.block_in, bf16[256,512]{1,0:T(8,128)(2,1)S(1)} %get-tuple-element.12.grad_v, bf16[256,128]{1,0:T(8,128)(2,1)S(1)} %get-tuple-element.13.full), custom_call_target="tpu_custom_call" | custom-call | tf_op jit(solution)/shard_map/finish/pallas_call | solution.py:563

commit v3 on v2

--- a/solution.py
+++ b/solution.py
@@ -11,7 +11,7 @@
 SPACE = 128
 DP = 4
 GROUP = 8
-ZS = 16
+PAIRS = 8
 COLS = 5
 ROWS = 256
 LANES = 512
@@ -19,9 +19,9 @@
 TILES = 14
 PACKED = 224
 PADDED = 256
-PIECE = 32
+PIECE = 16
 NEAR = (1, 2, SPACE - 1, SPACE - 2)
-RS_ORDER = [(dx, dg) for dx in (2, 1, 3, 0) for dg in (4, 5, 3, 2, 6, 7, 1, 0) if (dx, dg) != (0, 0)]
+BLOCK = [(ds, dg) for dg in (4, 5, 3, 2, 6, 7, 1, 0) for ds in (1, 0) if (ds, dg) != (0, 0)]
 XY_LINKS = ((0, 1), (2, 3), (6, 7), (8, 9))
 
 
@@ -74,21 +74,37 @@
 def face_copies(send_xy, send_z, recv_xy, recv_z, sems):
     me = lax.axis_index("space")
     copies = []
-    for n, step in enumerate(NEAR):
+    for step in NEAR:
         column = near_column(step)
-        peer = lax.rem(me + step, SPACE)
         for m, (src, dst) in enumerate(((send_xy, recv_xy), (send_z, recv_z))):
             copies.append(
                 pltpu.make_async_remote_copy(
                     src_ref=src.at[column],
                     dst_ref=dst.at[column],
-                    send_sem=sems.at[0, 2 * n + m],
-                    recv_sem=sems.at[1, 2 * n + m],
-                    device_id={"space": peer},
+                    send_sem=sems.at[0, m],
+                    recv_sem=sems.at[1, m],
+                    device_id={"space": lax.rem(me + step, SPACE)},
                     device_id_type=MESH,
                 )
             )
     return copies
+
+
+def wait_bytes(view, send_sem, recv_sem):
+    peer = lax.rem(lax.axis_index("space") + 1, SPACE)
+    pltpu.make_async_remote_copy(
+        src_ref=view,
+        dst_ref=view,
+        send_sem=send_sem,
+        recv_sem=recv_sem,
+        device_id={"space": peer},
+        device_id_type=MESH,
+    ).wait()
+
+
+def wait_faces(recv_xy, recv_z, sems):
+    wait_bytes(recv_xy.at[pl.ds(0, 4)], sems.at[0, 0], sems.at[1, 0])
+    wait_bytes(recv_z.at[pl.ds(0, 4)], sems.at[0, 1], sems.at[1, 1])
 
 
 def own_faces(send_xy, send_z, recv_xy, recv_z):
@@ -112,19 +128,23 @@
             wsend[64 * n + 16 * m : 64 * n + 16 * m + 16, :] = both.astype(BF16)
 
 
-def expand_mask(occ, cnt):
+def mask_parts():
     place = lax.broadcasted_iota(jnp.int32, (64, LANES), 1)
     owner = (place >> 3) == lax.broadcasted_iota(jnp.int32, (64, LANES), 0)
+    fold = lax.broadcasted_iota(jnp.int32, (LANES, 128), 0) & 7
+    fold = (fold == lax.broadcasted_iota(jnp.int32, (LANES, 128), 1)).astype(F32).astype(BF16)
+    widen = lax.broadcasted_iota(jnp.int32, (128, LANES), 1) >> 6
+    widen = (widen == lax.broadcasted_iota(jnp.int32, (128, LANES), 0)).astype(F32).astype(BF16)
+    return owner.astype(F32), fold, widen
+
+
+def expand_mask(occ, cnt, owner, fold, widen):
     spread = []
     for b in range(4):
         live = jnp.minimum(jnp.maximum(cnt[0, 0] - b, 0), 1)
         row = (occ[b : b + 1, :] * live).astype(F32)
-        spread.append(jnp.where(owner, jnp.broadcast_to(row, (64, LANES)), 0.0))
-    fold = lax.broadcasted_iota(jnp.int32, (LANES, 128), 0) & 7
-    fold = (fold == lax.broadcasted_iota(jnp.int32, (LANES, 128), 1)).astype(F32).astype(BF16)
+        spread.append(owner * jnp.broadcast_to(row, (64, LANES)))
     by_z = jnp.dot(jnp.concatenate(spread, axis=0).astype(BF16), fold, preferred_element_type=F32)
-    widen = lax.broadcasted_iota(jnp.int32, (128, LANES), 1) >> 6
-    widen = (widen == lax.broadcasted_iota(jnp.int32, (128, LANES), 0)).astype(F32).astype(BF16)
     return jnp.dot(by_z.astype(BF16), widen, preferred_element_type=F32)
 
 
@@ -260,13 +280,18 @@
 ):
     me, part = lax.axis_index("space"), lax.axis_index("dp")
     zed, spot = me // GROUP, lax.rem(me, GROUP)
+    pair, side = zed // 2, lax.rem(zed, 2)
     barrier = pltpu.get_barrier_semaphore()
 
     def in_group(d):
         return {"space": zed * GROUP + lax.rem(spot + d, GROUP)}
 
     def along_z(d):
-        return {"space": lax.rem(zed + d, ZS) * GROUP + spot}
+        return {"space": lax.rem(zed + d, 2 * PAIRS) * GROUP + spot}
+
+    def in_block(ds, dg):
+        to = lax.rem(side + ds, 2), lax.rem(spot + dg, GROUP)
+        return (2 * pair + to[0]) * GROUP + to[1], to[0] * GROUP + to[1]
 
     def along_dp(d):
         return {"dp": lax.rem(part + d, DP)}
@@ -276,10 +301,10 @@
             pl.semaphore_signal(sem, inc=1, device_id=peer, device_id_type=MESH)
 
     across = [along_dp(d) for d in range(1, DP)]
-    beside = [along_z(1), along_z(ZS - 1)]
+    beside = [along_z(1), along_z(2 * PAIRS - 1)]
     near = [{"space": lax.rem(me + step, SPACE)} for step in NEAR]
-    near += across + beside + [in_group(d) for d in range(1, GROUP)]
-    tell(barrier, near)
+    around = [in_group(d) for d in range(1, GROUP)]
+    near += across + beside + around
     loads = [
         pltpu.make_async_copy(far, here, in_sems.at[n])
         for n, (far, here) in enumerate(
@@ -291,9 +316,14 @@
     ]
     for load in loads:
         load.start()
-
+    tell(barrier, near)
+
+    constants = mask_parts()
+    for n in (2, 3):
+        loads[n].wait()
+    pack_weights(wt_v, bias_v, wsend)
     loads[0].wait()
-    active = expand_mask(occ_v, cnt)
+    active = expand_mask(occ_v, cnt, *constants)
     mask[...] = active.astype(BF16)
     loads[1].wait()
     values = feat_v[...].astype(F32) * active
@@ -301,9 +331,6 @@
         keep(src, flat, sides, q, values[:, 128 * q : 128 * q + 128])
     loads[5].wait()
     pack_faces(src, sides, snd, send_xy, send_z)
-    loads[2].wait()
-    loads[3].wait()
-    pack_weights(wt_v, bias_v, wsend)
 
     pl.semaphore_wait(barrier, len(near))
     copies = face_copies(send_xy, send_z, recv_xy, recv_z, sems)
@@ -311,8 +338,8 @@
         pltpu.make_async_remote_copy(
             src_ref=wsend,
             dst_ref=wall.at[part],
-            send_sem=wsems.at[0, d],
-            recv_sem=wsems.at[1, d],
+            send_sem=wsems.at[0],
+            recv_sem=wsems.at[1],
             device_id=along_dp(d),
             device_id_type=MESH,
         )
@@ -320,19 +347,17 @@
     ]
     for copy in copies + shares:
         copy.start()
-    tell(ready.at[0], across + beside)
+    tell(ready.at[0], across + beside + around)
     wall[part] = wsend[...]
     own_faces(send_xy, send_z, recv_xy, recv_z)
     u_xy[0:8] = jnp.zeros((8, 8, LANES), F32)
     u_z[0:2] = jnp.zeros((2, 64, 128), F32)
-    for copy in shares:
-        copy.wait()
+    wait_bytes(wall.at[pl.ds(0, DP - 1)], wsems.at[0], wsems.at[1])
     build_bands(wall, both, forward, backward)
     bias_row = whole_bias(wall)
-    for copy in copies:
-        copy.wait()
-    pl.semaphore_wait(ready.at[0], len(across) + len(beside))
-    tell(ready.at[1], [along_z(2), along_z(ZS - 2)])
+    wait_faces(recv_xy, recv_z, sems)
+    pl.semaphore_wait(ready.at[0], len(across) + len(beside) + len(around))
+    tell(ready.at[1], across + [along_z(2), along_z(2 * PAIRS - 2)])
 
     loads[6].wait()
     read_units(recv_xy, recv_z, u_xy, u_z)
@@ -353,60 +378,62 @@
         keep(src, flat, sides, p, g)
         turned[:, 256 * p : 256 * p + 256] = g.T.astype(BF16)
         bias_sum += jnp.sum(g, axis=0, keepdims=True)
+    pl.semaphore_wait(ready.at[1], len(across) + 2)
+    tell(ready.at[2], [along_z(4), along_z(2 * PAIRS - 4)])
+
+    low = low_half((16, 128))
+    top_row = lax.broadcasted_iota(jnp.int32, (16, 128), 0) == 0
+    bias_sum = bias_sum + swap_halves(bias_sum)
+    bias_tile = jnp.where(top_row, jnp.broadcast_to(bias_sum, (16, 128)), 0.0)
+
+    def reduce_copy(i, ds, dg):
+        to, place = in_block(ds, dg)
+        at = 2 * GROUP * lax.rem(i - part + DP, DP) + GROUP * ds + dg
+        return pltpu.make_async_remote_copy(
+            src_ref=packed.at[i, pl.ds(pl.multiple_of(place * PIECE, PIECE), PIECE)],
+            dst_ref=rs_recv.at[at],
+            send_sem=rs_sems.at[0],
+            recv_sem=rs_sems.at[1],
+            device_id={"space": to, "dp": i},
+            device_id_type=MESH,
+        )
+
+    done = 0
+    for owners, upto in (((0,), 3), ((1,), 5), ((2,), 7), ((3,), 9)):
+        for t in range(done, upto):
+            r = jnp.dot(
+                turned[...], columns[:, 256 * t : 256 * t + 256], preferred_element_type=F32
+            ).T
+            r0, r1, r2, r3 = (r[64 * n : 64 * n + 64, :] for n in range(4))
+            row = 192 * t
+            sums[row : row + 64, :] = r3 + swap_halves(r0)
+            sums[row + 64 : row + 128, :] = r0 + swap_halves(r1)
+            sums[row + 128 : row + 192, :] = r1 + swap_halves(r2)
+        done = upto
+        for i in owners:
+            for m in range(TILES):
+                row = 16 * (27 * i + 2 * m)
+                if m < TILES - 1:
+                    other = swap_halves(sums[row + 16 : row + 32, :])
+                else:
+                    other = bias_tile
+                tile = jnp.where(low, sums[row : row + 16, :], other)
+                packed[i, 16 * m : 16 * m + 16, :] = tile.astype(BF16)
+            packed[i, PACKED:PADDED, :] = jnp.zeros((PADDED - PACKED, 128), BF16)
+        for i in owners:
+            for ds, dg in BLOCK:
+                reduce_copy(i, ds, dg).start()
+        for i in owners:
+
+            @pl.when(part != i)
+            def _(i=i):
+                reduce_copy(i, 0, 0).start()
+
     pack_faces(src, sides, snd, send_gxy, send_gz)
-
     face = face_copies(send_gxy, send_gz, recv_gxy, recv_gz, gsems)
     for copy in face:
         copy.start()
     own_faces(send_gxy, send_gz, recv_gxy, recv_gz)
-    pl.semaphore_wait(ready.at[1], 2)
-    tell(ready.at[2], [along_z(4), along_z(ZS - 4)])
-
-    for t in range(9):
-        r = jnp.dot(
-            turned[...], columns[:, 256 * t : 256 * t + 256], preferred_element_type=F32
-        ).T
-        r0, r1, r2, r3 = (r[64 * n : 64 * n + 64, :] for n in range(4))
-        row = 192 * t
-        sums[row : row + 64, :] = r3 + swap_halves(r0)
-        sums[row + 64 : row + 128, :] = r0 + swap_halves(r1)
-        sums[row + 128 : row + 192, :] = r1 + swap_halves(r2)
-    low = low_half((16, 128))
-    top_row = lax.broadcasted_iota(jnp.int32, (16, 128), 0) == 0
-    bias_sum = bias_sum + swap_halves(bias_sum)
-    bias_tile = jnp.where(top_row, jnp.broadcast_to(bias_sum, (16, 128)), 0.0)
-    for i in range(DP):
-        for m in range(TILES):
-            row = 16 * (27 * i + 2 * m)
-            if m < TILES - 1:
-                other = swap_halves(sums[row + 16 : row + 32, :])
-            else:
-                other = bias_tile
-            tile = jnp.where(low, sums[row : row + 16, :], other)
-            packed[i, 16 * m : 16 * m + 16, :] = tile.astype(BF16)
-        packed[i, PACKED:PADDED, :] = jnp.zeros((PADDED - PACKED, 128), BF16)
-
-    rs_copies = []
-    for dx, dg in RS_ORDER:
-        to = lax.rem(part + dx, DP), lax.rem(spot + dg, GROUP)
-        at = 8 * dx + dg
-        rs_copies.append(
-            pltpu.make_async_remote_copy(
-                src_ref=packed.at[to[0], pl.ds(pl.multiple_of(to[1] * PIECE, PIECE), PIECE)],
-                dst_ref=rs_recv.at[at],
-                send_sem=rs_sems.at[0, at],
-                recv_sem=rs_sems.at[1, at],
-                device_id={"space": zed * GROUP + to[1], "dp": to[0]},
-                device_id_type=MESH,
-            )
-        )
-    for copy in rs_copies:
-        copy.start()
-
-    for copy in face:
-        copy.wait()
-    read_units(recv_gxy, recv_gz, u_xy, u_z)
-    build_columns(src, nbr, u_xy, u_z, stage, columns)
 
     def grad_input(p):
         lanes = slice(128 * p, 128 * p + 128)
@@ -418,51 +445,43 @@
         )
         grad_in[:, lanes] = (r * mask[:, lanes].astype(F32)).astype(BF16)
 
-    for copy in rs_copies:
-        copy.wait()
-    mine = pl.ds(pl.multiple_of(spot * PIECE, PIECE), PIECE)
+    wait_bytes(rs_recv.at[pl.ds(1, 2 * DP * GROUP - 1)], rs_sems.at[0], rs_sems.at[1])
+    mine = pl.ds(pl.multiple_of((side * GROUP + spot) * PIECE, PIECE), PIECE)
     total = packed[part, mine, :].astype(F32)
-    for at in range(1, DP * GROUP):
+    for at in range(1, 2 * DP * GROUP):
         total += rs_recv[at].astype(F32)
-    z_recv[zed] = total.astype(BF16)
+    z_recv[pair] = total.astype(BF16)
     pl.semaphore_wait(ready.at[2], 2)
-    z_copies = [
+    for d in (4, 3, 5, 2, 6, 1, 7):
         pltpu.make_async_remote_copy(
-            src_ref=z_recv.at[zed],
-            dst_ref=z_recv.at[zed],
-            send_sem=z_sems.at[0, d],
-            recv_sem=z_sems.at[1, d],
-            device_id=along_z(d),
+            src_ref=z_recv.at[pair],
+            dst_ref=z_recv.at[pair],
+            send_sem=z_sems.at[0],
+            recv_sem=z_sems.at[1],
+            device_id={"space": (2 * lax.rem(pair + d, PAIRS) + side) * GROUP + spot},
             device_id_type=MESH,
-        )
-        for d in (8, 7, 9, 6, 10, 5, 11, 4, 12, 3, 13, 2, 14, 1, 15)
-    ]
-    for copy in z_copies:
-        copy.start()
+        ).start()
+    wait_faces(recv_gxy, recv_gz, gsems)
+    read_units(recv_gxy, recv_gz, u_xy, u_z)
+    build_columns(src, nbr, u_xy, u_z, stage, columns)
     for p in range(4):
         grad_input(p)
 
-    for copy in z_copies:
-        copy.wait()
+    wait_bytes(z_recv.at[pl.ds(0, PAIRS - 1)], z_sems.at[0], z_sems.at[1])
     total = z_recv[0].astype(F32)
-    for d in range(1, ZS):
+    for d in range(1, PAIRS):
         total += z_recv[d].astype(F32)
     full[mine, :] = total.astype(BF16)
-    ag_copies = [
+    for ds, dg in BLOCK:
         pltpu.make_async_remote_copy(
             src_ref=full.at[mine],
             dst_ref=full.at[mine],
-            send_sem=ag_sems.at[0, d],
-            recv_sem=ag_sems.at[1, d],
-            device_id=in_group(d),
+            send_sem=ag_sems.at[0],
+            recv_sem=ag_sems.at[1],
+            device_id={"space": in_block(ds, dg)[0]},
             device_id_type=MESH,
-        )
-        for d in range(1, GROUP)
-    ]
-    for copy in ag_copies:
-        copy.start()
-    for copy in ag_copies:
-        copy.wait()
+        ).start()
+    wait_bytes(full.at[pl.ds(0, (2 * GROUP - 1) * PIECE)], ag_sems.at[0], ag_sems.at[1])
 
 
 def last_kernel(block_in, grad_v, full, block_out, grad_out, gw, gb, rows):
@@ -535,15 +554,15 @@
             pltpu.VMEM((128, 1024), BF16),
             pltpu.VMEM((1728, 128), F32),
             pltpu.VMEM((DP, PADDED, 128), BF16),
-            pltpu.VMEM((DP * GROUP, PIECE, 128), BF16),
-            pltpu.VMEM((ZS, PIECE, 128), BF16),
+            pltpu.VMEM((2 * DP * GROUP, PIECE, 128), BF16),
+            pltpu.VMEM((PAIRS, PIECE, 128), BF16),
             pltpu.SemaphoreType.DMA((7,)),
-            pltpu.SemaphoreType.DMA((2, 8)),
-            pltpu.SemaphoreType.DMA((2, 8)),
-            pltpu.SemaphoreType.DMA((2, DP)),
-            pltpu.SemaphoreType.DMA((2, DP * GROUP)),
-            pltpu.SemaphoreType.DMA((2, ZS)),
-            pltpu.SemaphoreType.DMA((2, GROUP)),
+            pltpu.SemaphoreType.DMA((2, 2)),
+            pltpu.SemaphoreType.DMA((2, 2)),
+            pltpu.SemaphoreType.DMA((2,)),
+            pltpu.SemaphoreType.DMA((2,)),
+            pltpu.SemaphoreType.DMA((2,)),
+            pltpu.SemaphoreType.DMA((2,)),
             pltpu.SemaphoreType.REGULAR((3,)),
         ],
         compiler_params=pltpu.CompilerParams(

time: 48.8 us -> 45.5 us (0.932)
  the two profiles are of different devices: /device:TPU:1 before, /device:TPU:6 now
where the time goes in v3:
time: 45.5 us; the launch traced here: 45.3 us
  Pallas kernels  44 us (97%)
  between operations  1.29 us (3%)
    pallas_call x1, Pallas kernels, body(): pl.pallas_call(main_kernel, out_shape=(of((ROWS, LANES), BF16), of((ROWS,...  43.1 us
    pallas_call x1, Pallas kernels, body(): pl.pallas_call(last_kernel, out_shape=(of((ROWS, LANES), BF16), of((ROWS,...  0.99 us

profile of v3, /device:TPU:6, one launch (start us, length us, event | category | flops | bytes accessed | tf_op | source)
XLA Modules:
  0.0 45.3 jit_solution(6310152642125389456)
XLA Ops:
  1.3 43.1 %main.1 = (bf16[256,512]{1,0:T(8,128)(2,1)S(1)}, bf16[256,512]{1,0:T(8,128)(2,1)S(1)}, bf16[256,128]{1,0:T(8,128)(2,1)S(1)}) custom-call(s32[1,1]{1,0:T(1,128)S(6)} %copy.12.cnt, bf16[256,512]{1,0:T(8,128)(2,1)} %bitcast.11, s32[4,512]{1,0:T(4,128)} %bitcast.14, bf16[64,432]{1,0:T(8,128)(2,1)} %bitcast.13, bf16[1,16]{1,0:T(2,128)(2,1)} %bitcast.17, ...), custom_call_target="tpu_custom_call" | custom-call | tf_op jit(solution)/shard_map/main/pallas_call | solution.py:525
  44.3 1.0 %finish.1 = (bf16[256,512]{1,0:T(8,128)(2,1)}, bf16[256,512]{1,0:T(8,128)(2,1)}, f32[64,432]{1,0:T(8,128)}, f32[1,16]{1,0:T(1,128)}) custom-call(bf16[256,512]{1,0:T(8,128)(2,1)S(1)} %get-tuple-element.11.block_in, bf16[256,512]{1,0:T(8,128)(2,1)S(1)} %get-tuple-element.12.grad_v, bf16[256,128]{1,0:T(8,128)(2,1)S(1)} %get-tuple-element.13.full), custom_call_target="tpu_custom_call" | custom-call | tf_op jit(solution)/shard_map/finish/pallas_call | solution.py:582

commit v4 on v3

--- a/solution.py
+++ b/solution.py
@@ -90,16 +90,20 @@
     return copies
 
 
-def wait_bytes(view, send_sem, recv_sem):
+def copies_of(view, send_sem, recv_sem):
     peer = lax.rem(lax.axis_index("space") + 1, SPACE)
-    pltpu.make_async_remote_copy(
+    return pltpu.make_async_remote_copy(
         src_ref=view,
         dst_ref=view,
         send_sem=send_sem,
         recv_sem=recv_sem,
         device_id={"space": peer},
         device_id_type=MESH,
-    ).wait()
+    )
+
+
+def wait_bytes(view, send_sem, recv_sem):
+    copies_of(view, send_sem, recv_sem).wait()
 
 
 def wait_faces(recv_xy, recv_z, sems):
@@ -156,7 +160,7 @@
         u_z[2 * column + 2 : 2 * column + 4] = planes.reshape(2, 64, 128)
 
 
-def build_columns(src, nbr, u_xy, u_z, stage, columns):
+def build_columns(src, nbr, u_xy, u_z, columns):
     low = low_half((8, 128))
     low_row = low_half((1, 128))
     depth = lax.broadcasted_iota(jnp.int32, (8, 640), 0)
@@ -215,19 +219,21 @@
             c = jnp.concatenate([here, jnp.where(low, after, before)], axis=1)
             down = jnp.where(depth == 0, jnp.broadcast_to(lower, (8, 640)), pltpu.roll(c, 1, axis=0))
             up = jnp.where(depth == 7, jnp.broadcast_to(upper, (8, 640)), pltpu.roll(c, 7, axis=0))
-            for e, tile in enumerate((down, c, up)):
-                stage[e, 8 * xx : 8 * xx + 8, :] = expand(tile)
-        for a in range(3):
-            for e in range(3):
-                t = 3 * a + e
-                for p in range(4):
-                    rows = pl.ds(pl.multiple_of(b * 64, 64) + 256 * p, 64)
-                    columns[rows, 256 * t : 256 * t + 256] = stage[
-                        e, 8 * a : 8 * a + 64, 256 * p : 256 * p + 256
-                    ].astype(BF16)
+            tiles = [expand(tile) for tile in (down, c, up)]
+            for e in range(3) if xx else ():
+                pair = jnp.concatenate([before_tiles[e], tiles[e]], axis=0).astype(BF16)
+                for a in range(3):
+                    x = xx - 1 - a
+                    if x not in (0, 2, 4, 6):
+                        continue
+                    lane = 256 * (3 * a + e)
+                    for p in range(4):
+                        rows = pl.ds(pl.multiple_of(b * 64, 64) + 256 * p + 8 * x, 16)
+                        columns[rows, lane : lane + 256] = pair[:, 256 * p : 256 * p + 256]
+            before_tiles = tiles
         return carry
 
-    lax.fori_loop(0, 4, one_brick, 0)
+    lax.fori_loop(0, 4, one_brick, 0, unroll=True)
 
 
 def build_bands(wall, both, forward, backward):
@@ -273,7 +279,7 @@
     cnt, feat, occ, wt, bias, cot, snd_in, nbr_in,
     block_out, grad_in, full,
     snd, nbr, feat_v, occ_v, wt_v, bias_v, cot_v, mask, wsend, wall,
-    src, u_xy, u_z, stage, columns, both, forward, backward,
+    src, u_xy, u_z, columns, both, forward, backward,
     flat, sides, send_xy, send_z, recv_xy, recv_z, send_gxy, send_gz, recv_gxy, recv_gz, turned,
     sums, packed, rs_recv, z_recv,
     in_sems, sems, gsems, wsems, rs_sems, z_sems, ag_sems, ready,
@@ -314,14 +320,11 @@
             )
         )
     ]
-    for load in loads:
-        load.start()
+    for n in (0, 1, 2, 3, 5):
+        loads[n].start()
     tell(barrier, near)
 
     constants = mask_parts()
-    for n in (2, 3):
-        loads[n].wait()
-    pack_weights(wt_v, bias_v, wsend)
     loads[0].wait()
     active = expand_mask(occ_v, cnt, *constants)
     mask[...] = active.astype(BF16)
@@ -332,8 +335,14 @@
     loads[5].wait()
     pack_faces(src, sides, snd, send_xy, send_z)
 
+    for n in (4, 6):
+        loads[n].start()
     pl.semaphore_wait(barrier, len(near))
-    copies = face_copies(send_xy, send_z, recv_xy, recv_z, sems)
+    for copy in face_copies(send_xy, send_z, recv_xy, recv_z, sems):
+        copy.start()
+    for n in (2, 3):
+        loads[n].wait()
+    pack_weights(wt_v, bias_v, wsend)
     shares = [
         pltpu.make_async_remote_copy(
             src_ref=wsend,
@@ -345,7 +354,7 @@
         )
         for d in range(1, DP)
     ]
-    for copy in copies + shares:
+    for copy in shares:
         copy.start()
     tell(ready.at[0], across + beside + around)
     wall[part] = wsend[...]
@@ -361,7 +370,7 @@
 
     loads[6].wait()
     read_units(recv_xy, recv_z, u_xy, u_z)
-    build_columns(src, nbr, u_xy, u_z, stage, columns)
+    build_columns(src, nbr, u_xy, u_z, columns)
     loads[4].wait()
     bias_sum = jnp.zeros((1, 128), F32)
     for p in range(4):
@@ -423,17 +432,15 @@
         for i in owners:
             for ds, dg in BLOCK:
                 reduce_copy(i, ds, dg).start()
-        for i in owners:
-
-            @pl.when(part != i)
-            def _(i=i):
-                reduce_copy(i, 0, 0).start()
+    for d in range(1, DP):
+        reduce_copy(lax.rem(part + d, DP), 0, 0).start()
 
     pack_faces(src, sides, snd, send_gxy, send_gz)
-    face = face_copies(send_gxy, send_gz, recv_gxy, recv_gz, gsems)
-    for copy in face:
+    own_faces(send_gxy, send_gz, recv_gxy, recv_gz)
+    reduced = copies_of(rs_recv.at[pl.ds(1, 2 * DP * GROUP - 1)], rs_sems.at[0], rs_sems.at[1])
+    reduced.wait_send()
+    for copy in face_copies(send_gxy, send_gz, recv_gxy, recv_gz, gsems):
         copy.start()
-    own_faces(send_gxy, send_gz, recv_gxy, recv_gz)
 
     def grad_input(p):
         lanes = slice(128 * p, 128 * p + 128)
@@ -445,7 +452,7 @@
         )
         grad_in[:, lanes] = (r * mask[:, lanes].astype(F32)).astype(BF16)
 
-    wait_bytes(rs_recv.at[pl.ds(1, 2 * DP * GROUP - 1)], rs_sems.at[0], rs_sems.at[1])
+    reduced.wait_recv()
     mine = pl.ds(pl.multiple_of((side * GROUP + spot) * PIECE, PIECE), PIECE)
     total = packed[part, mine, :].astype(F32)
     for at in range(1, 2 * DP * GROUP):
@@ -463,7 +470,7 @@
         ).start()
     wait_faces(recv_gxy, recv_gz, gsems)
     read_units(recv_gxy, recv_gz, u_xy, u_z)
-    build_columns(src, nbr, u_xy, u_z, stage, columns)
+    build_columns(src, nbr, u_xy, u_z, columns)
     for p in range(4):
         grad_input(p)
 
@@ -541,7 +548,6 @@
             pltpu.VMEM((4, 40, 8, 128), F32),
             pltpu.VMEM((48, 8, LANES), F32),
             pltpu.VMEM((12, 64, 128), F32),
-            pltpu.VMEM((3, 80, 1024), F32),
             pltpu.VMEM((1024, WIDE), BF16),
             pltpu.VMEM((1728, 128), F32),
             pltpu.VMEM((WIDE, 128), BF16),

time: 45.5 us -> 43.1 us (0.947)
  the two profiles are of different devices: /device:TPU:6 before, /device:TPU:1 now
where the time goes in v4:
time: 43.1 us; the launch traced here: 42.9 us
  Pallas kernels  41.6 us (97%)
  between operations  1.29 us (3%)
    pallas_call x1, Pallas kernels, body(): pl.pallas_call(main_kernel, out_shape=(of((ROWS, LANES), BF16), of((ROWS,...  40.6 us
    pallas_call x1, Pallas kernels, body(): pl.pallas_call(last_kernel, out_shape=(of((ROWS, LANES), BF16), of((ROWS,...  0.99 us

profile of v4, /device:TPU:1, one launch (start us, length us, event | category | flops | bytes accessed | tf_op | source)
XLA Modules:
  0.0 42.9 jit_solution(6279739091089500880)
XLA Ops:
  1.3 40.6 %main.1 = (bf16[256,512]{1,0:T(8,128)(2,1)S(1)}, bf16[256,512]{1,0:T(8,128)(2,1)S(1)}, bf16[256,128]{1,0:T(8,128)(2,1)S(1)}) custom-call(s32[1,1]{1,0:T(1,128)S(6)} %copy.12.cnt, bf16[256,512]{1,0:T(8,128)(2,1)} %bitcast.11, s32[4,512]{1,0:T(4,128)} %bitcast.14, bf16[64,432]{1,0:T(8,128)(2,1)} %bitcast.13, bf16[1,16]{1,0:T(2,128)(2,1)} %bitcast.17, ...), custom_call_target="tpu_custom_call" | custom-call | tf_op jit(solution)/shard_map/main/pallas_call | solution.py:532
  41.9 1.0 %finish.1 = (bf16[256,512]{1,0:T(8,128)(2,1)}, bf16[256,512]{1,0:T(8,128)(2,1)}, f32[64,432]{1,0:T(8,128)}, f32[1,16]{1,0:T(1,128)}) custom-call(bf16[256,512]{1,0:T(8,128)(2,1)S(1)} %get-tuple-element.11.block_in, bf16[256,512]{1,0:T(8,128)(2,1)S(1)} %get-tuple-element.12.grad_v, bf16[256,128]{1,0:T(8,128)(2,1)S(1)} %get-tuple-element.13.full), custom_call_target="tpu_custom_call" | custom-call | tf_op jit(solution)/shard_map/finish/pallas_call | solution.py:588

commit v5 on v4

--- a/solution.py
+++ b/solution.py
@@ -387,8 +387,6 @@
         keep(src, flat, sides, p, g)
         turned[:, 256 * p : 256 * p + 256] = g.T.astype(BF16)
         bias_sum += jnp.sum(g, axis=0, keepdims=True)
-    pl.semaphore_wait(ready.at[1], len(across) + 2)
-    tell(ready.at[2], [along_z(4), along_z(2 * PAIRS - 4)])
 
     low = low_half((16, 128))
     top_row = lax.broadcasted_iota(jnp.int32, (16, 128), 0) == 0
@@ -429,6 +427,9 @@
                 tile = jnp.where(low, sums[row : row + 16, :], other)
                 packed[i, 16 * m : 16 * m + 16, :] = tile.astype(BF16)
             packed[i, PACKED:PADDED, :] = jnp.zeros((PADDED - PACKED, 128), BF16)
+        if 0 in owners:
+            pl.semaphore_wait(ready.at[1], len(across) + 2)
+            tell(ready.at[2], [along_z(4), along_z(2 * PAIRS - 4)])
         for i in owners:
             for ds, dg in BLOCK:
                 reduce_copy(i, ds, dg).start()

time: 43.1 us -> 42.7 us (level)
  no operation moved by 1% of the time
where the time goes in v5:
time: 42.7 us; the launch traced here: 42.5 us
  Pallas kernels  41.2 us (96%)
  between operations  1.29 us (3%)
    pallas_call x1, Pallas kernels, body(): pl.pallas_call(main_kernel, out_shape=(of((ROWS, LANES), BF16), of((ROWS,...  40.3 us
    pallas_call x1, Pallas kernels, body(): pl.pallas_call(last_kernel, out_shape=(of((ROWS, LANES), BF16), of((ROWS,...  0.99 us

profile of v5, /device:TPU:1, one launch (start us, length us, event | category | flops | bytes accessed | tf_op | source)
XLA Modules:
  0.0 42.5 jit_solution(4888858831395574407)
XLA Ops:
  1.3 40.3 %main.1 = (bf16[256,512]{1,0:T(8,128)(2,1)S(1)}, bf16[256,512]{1,0:T(8,128)(2,1)S(1)}, bf16[256,128]{1,0:T(8,128)(2,1)S(1)}) custom-call(s32[1,1]{1,0:T(1,128)S(6)} %copy.12.cnt, bf16[256,512]{1,0:T(8,128)(2,1)} %bitcast.11, s32[4,512]{1,0:T(4,128)} %bitcast.14, bf16[64,432]{1,0:T(8,128)(2,1)} %bitcast.13, bf16[1,16]{1,0:T(2,128)(2,1)} %bitcast.17, ...), custom_call_target="tpu_custom_call" | custom-call | tf_op jit(solution)/shard_map/main/pallas_call | solution.py:533
  41.5 1.0 %finish.1 = (bf16[256,512]{1,0:T(8,128)(2,1)}, bf16[256,512]{1,0:T(8,128)(2,1)}, f32[64,432]{1,0:T(8,128)}, f32[1,16]{1,0:T(1,128)}) custom-call(bf16[256,512]{1,0:T(8,128)(2,1)S(1)} %get-tuple-element.11.block_in, bf16[256,512]{1,0:T(8,128)(2,1)S(1)} %get-tuple-element.12.grad_v, bf16[256,128]{1,0:T(8,128)(2,1)S(1)} %get-tuple-element.13.full), custom_call_target="tpu_custom_call" | custom-call | tf_op jit(solution)/shard_map/finish/pallas_call | solution.py:589
